TPU v7x, 128 devices: a whole 4x4x4 slice. The times are simulated.
128 devices in a mesh: dp: 16 (over z, x), head: 8 (over y, core).
Axes of the slice: x: 4, y: 4, z: 4, core: 2. Of those that a mesh axis runs over, the one named last changes fastest.
Arguments:
- prefill_query: bfloat16 [16384, 8192], P(('dp', 'head')), may hold values from -20 to 20
- prefill_pairs: bfloat16 [16384, 2048], P(('dp', 'head')), may hold values from -4 to 4
- decode_query: bfloat16 [128, 8192], P(('dp', 'head')), may hold values from -20 to 20
- decode_pairs: bfloat16 [128, 2048], P(('dp', 'head')), may hold values from -4 to 4
- cache_pool: bfloat16 [2560, 8, 64, 256], P('dp', 'head'), may hold values from -11 to 11
- decode_pages: int32 [128, 16], P('dp'), may hold values from 0 to 159, as said below
- prefill_pages: int32 [16, 32], P('dp'), may hold values from 0 to 159, as said below
- cache_length: int32 [128], replicated, may hold values from 1 to 1023, as said below
- prefix_length: int32 [16], P('dp'), may hold values from 0 to 1024, as said below
- migrant_slot: int32 [16, 1], replicated, may hold values from 0 to 7, as said below
- migrant_target: int32 [16, 1], replicated, may hold values from 0 to 15, as said below
- arrivals: int32 [128], replicated, may hold values from 0 to 127, each once
Outputs:
- prefill_attended: bfloat16 [16384, 8192], P(('dp', 'head'))
- decode_attended: bfloat16 [128, 8192], P('dp', 'head')
- updated_pool: bfloat16 [2560, 8, 64, 256], P('dp', 'head')
Inputs may be any that keep to these rules, and one draw needn't show every extreme that they name: Page numbers within the group's pool; in each group the entries of its 8 rows of decode_pages and its row of prefill_pages are all different. `prefill_pages`: see decode_pages. `cache_length`: A migrating request holds at most 255 cached tokens, and one holds exactly 255. `prefix_length`: A multiple of 64. `migrant_slot`: the slots of one group are all different. `migrant_target`: each column is a permutation of the groups: every group receives exactly one request of each column; a request may stay in its group.
All inputs are finite; a program needn't handle non-finite values.
Results may differ from a plain program's by a relative error of at most 0.008.
Values may be sent and summed in bfloat16 or wider, within the bound.
A program may use at most 128 MiB of HBM per device.

v0:
```python
import jax
import jax.numpy as jnp
from jax import lax
from jax.sharding import PartitionSpec as P

HD = 128
PAGE = 64
MIGP = 4


big_negative = -1e30


def decode_attend(queries, key_pages, lengths, inv_scale):
    slot_count = queries.shape[0]
    local_heads = key_pages.shape[2]
    page_size = key_pages.shape[3]
    head_size = key_pages.shape[4] // 2
    per_group = queries.shape[1] // (local_heads * head_size)
    grouped = queries.reshape(slot_count, local_heads, per_group, head_size)
    scores = (
        jnp.einsum(
            "skqd,smkpd->skqmp",
            grouped,
            key_pages[..., :head_size],
            preferred_element_type=jnp.float32,
        )
        * inv_scale
    )
    position = (
        jnp.arange(key_pages.shape[1], dtype=jnp.int32)[:, None] * page_size
        + jnp.arange(page_size, dtype=jnp.int32)[None, :]
    )
    visible = position[None, None, None] <= lengths[:, None, None, None, None]
    masked = jnp.where(visible, scores, big_negative)
    row_top = jnp.max(masked, axis=(3, 4), keepdims=True)
    weights = jnp.where(visible, jnp.exp(masked - row_top), 0.0)
    weight_sum = jnp.sum(weights, axis=(3, 4))
    mixed_sum = jnp.einsum(
        "skqmp,smkpd->skqd",
        weights.astype(jnp.bfloat16),
        key_pages[..., head_size:],
        preferred_element_type=jnp.float32,
    )
    return (mixed_sum / weight_sum[..., None]).reshape(slot_count, -1).astype(jnp.bfloat16)


def prefill_block(queries, key_pages, limit, inv_scale):
    row_total = queries.shape[0]
    local_heads = key_pages.shape[1]
    page_size = key_pages.shape[2]
    head_size = key_pages.shape[3] // 2
    per_group = queries.shape[1] // (local_heads * head_size)
    grouped = queries.reshape(row_total, local_heads, per_group, head_size)
    scores = (
        jnp.einsum(
            "tkqd,mkpd->kqtmp",
            grouped,
            key_pages[..., :head_size],
            preferred_element_type=jnp.float32,
        )
        * inv_scale
    )
    position = (
        jnp.arange(key_pages.shape[0], dtype=jnp.int32)[:, None] * page_size
        + jnp.arange(page_size, dtype=jnp.int32)[None, :]
    )
    visible = position[None, None, None] <= limit[None, None, :, None, None]
    masked = jnp.where(visible, scores, big_negative)
    row_top = jnp.max(masked, axis=(3, 4), keepdims=True)
    weights = jnp.where(visible, jnp.exp(masked - row_top), 0.0)
    weight_sum = jnp.sum(weights, axis=(3, 4))
    mixed_sum = jnp.einsum(
        "kqtmp,mkpd->tkqd",
        weights.astype(jnp.bfloat16),
        key_pages[..., head_size:],
        preferred_element_type=jnp.float32,
    )
    return (
        (mixed_sum / weight_sum.transpose(2, 0, 1)[..., None])
        .reshape(row_total, -1)
        .astype(jnp.bfloat16)
    )


def per_device(
    prefill_query,
    prefill_pairs,
    decode_query,
    decode_pairs,
    cache_pool,
    decode_pages,
    prefill_pages,
    cache_length,
    prefix_length,
    migrant_slot,
    migrant_target,
    arrivals,
):
    inv_scale = HD ** (-0.5)
    my_group = lax.axis_index("dp")
    head_part = lax.axis_index("head")
    slot_count = decode_pages.shape[0]
    mig_count = migrant_slot.shape[1]
    local_heads = cache_pool.shape[1]
    query_width = decode_query.shape[1] // lax.axis_size("head")
    pair_width = decode_pairs.shape[1] // lax.axis_size("head")
    my_slots = migrant_slot[my_group]
    own_pages = decode_pages[my_slots][:, :MIGP]
    leaving = cache_pool[own_pages]
    flat_target = migrant_target.reshape(-1)
    shard_piece = lax.all_gather(leaving, "dp", axis=0, tiled=True)
    row_count = shard_piece.shape[0]
    row_index = jnp.arange(row_count, dtype=jnp.int32)
    chosen = jnp.logical_and(
        (flat_target == my_group)[:, None],
        (row_index % mig_count)[:, None] == jnp.arange(mig_count, dtype=jnp.int32)[None, :],
    )
    moved_pages = jnp.einsum(
        "nk,nabcd->kabcd",
        chosen.astype(jnp.bfloat16),
        shard_piece,
        preferred_element_type=jnp.float32,
    )
    arriving = moved_pages.astype(jnp.bfloat16)
    new_pool = cache_pool.at[own_pages.reshape(-1)].set(
        arriving.reshape((-1,) + cache_pool.shape[1:])
    )
    source_slot = (
        jnp.arange(migrant_target.shape[0], dtype=jnp.int32)[:, None] * slot_count + migrant_slot
    )
    incoming_len = jnp.sum(
        jnp.where(migrant_target == my_group, cache_length[source_slot], 0), axis=0
    )
    own_len = lax.dynamic_slice_in_dim(cache_length, my_group * slot_count, slot_count)
    lengths = own_len.at[my_slots].set(incoming_len)
    wanted = my_group * slot_count + jnp.arange(slot_count, dtype=jnp.int32)
    onehot = (wanted[:, None] == arrivals[None, :]).astype(jnp.bfloat16)
    query_cols = lax.dynamic_slice_in_dim(
        lax.all_gather(decode_query, ("dp", "head"), axis=0, tiled=True),
        head_part * query_width,
        query_width,
        1,
    )
    pair_cols = lax.dynamic_slice_in_dim(
        lax.all_gather(decode_pairs, ("dp", "head"), axis=0, tiled=True),
        head_part * pair_width,
        pair_width,
        1,
    )
    query_rows = jnp.dot(onehot, query_cols, preferred_element_type=jnp.float32)
    pair_rows = jnp.dot(onehot, pair_cols, preferred_element_type=jnp.float32)
    query_rows = query_rows.astype(jnp.bfloat16)
    pair_rows = pair_rows.astype(jnp.bfloat16)
    page_index = lengths // PAGE
    page_now = jnp.take_along_axis(decode_pages, page_index[:, None], axis=1)[:, 0]
    new_pool = new_pool.at[page_now, :, lengths % PAGE, :].set(
        pair_rows.reshape(slot_count, local_heads, 2 * HD)
    )
    decode_attended = decode_attend(query_rows, new_pool[decode_pages], lengths, inv_scale)
    query_all, pair_all = (
        lax.all_to_all(prefill_query, "head", split_axis=1, concat_axis=0, tiled=True),
        lax.all_to_all(prefill_pairs, "head", split_axis=1, concat_axis=0, tiled=True),
    )
    span_rows = query_all.shape[0]
    pre_table = prefill_pages[0]
    prefix = prefix_length[0]
    span_pages = pair_all.reshape(span_rows // PAGE, PAGE, local_heads, 2 * HD).transpose(
        0, 2, 1, 3
    )
    dest_pages = lax.dynamic_slice_in_dim(pre_table, prefix // PAGE, span_rows // PAGE)
    new_pool = new_pool.at[dest_pages].set(span_pages)
    key_pages = new_pool[pre_table]
    block_rows = min(128, span_rows)
    blocks = query_all.reshape(span_rows // block_rows, block_rows, query_width)
    limits = (prefix + jnp.arange(span_rows, dtype=jnp.int32)).reshape(
        span_rows // block_rows, block_rows
    )

    def attend_block(block_items):
        return prefill_block(block_items[0], key_pages, block_items[1], inv_scale)

    outputs = lax.map(attend_block, (blocks, limits))
    out_span = outputs.reshape(span_rows, query_width)
    prefill_attended = lax.all_to_all(out_span, "head", split_axis=0, concat_axis=1, tiled=True)
    return (prefill_attended, decode_attended, new_pool)


def solution(mesh):
    placed = (
        P(("dp", "head"), None),
        P(("dp", "head"), None),
        P(("dp", "head"), None),
        P(("dp", "head"), None),
        P("dp", "head", None, None),
        P("dp", None),
        P("dp", None),
        P(),
        P("dp"),
        P(),
        P(),
        P(),
    )
    return jax.shard_map(
        per_device,
        mesh=mesh,
        in_specs=placed,
        out_specs=(P(("dp", "head"), None), P("dp", "head"), P("dp", "head", None, None)),
        check_vma=False,
    )
```

profile of v0, /device:TPU:0, one launch (start us, length us, event | category | flops | bytes accessed | tf_op | source)
XLA Modules:
  0.0 206.9 jit_solution(15597287813363803023)
XLA Ops:
  7.3 5.8 %copy.75 = bf16[160,1,64,256]{3,2,1,0:T(8,128)(2,1)} copy(bf16[160,1,64,256]{3,2,1,0:T(8,128)(2,1)} %param.20) | data formatting | bytes 10485760
  14.5 3.7 %gather_fusion = bf16[4,64,256]{2,1,0:T(8,128)(2,1)} fusion(bf16[160,64,256]{2,1,0:T(8,128)(2,1)} %bitcast.221, s32[1024]{0:T(1024)S(1)} %pad_clamp_fusion.3), kind=kCustom, calls=%fused_computation | custom fusion | bytes 262160 | tf_op jit(solution)/shard_map/gather | solution.py:110
  19.0 4.7 %all-to-all-start.1 = ((bf16[128,8,256]{2,0,1:T(8,128)(2,1)}), bf16[128,8,256]{2,0,1:T(8,128)(2,1)S(1)}, u32[]{:S(2)}, u32[]{:S(2)}) async-start(bf16[128,8,256]{2,0,1:T(8,128)(2,1)} %bitcast.188), calls=%async_computation.1 | async-start | bytes 1048576 | tf_op jit(solution)/shard_map/all_to_all | solution.py:163
  26.6 2.1 %fusion.61 = s32[8]{0:T(128)S(1)} fusion(s32[8]{0:T(128)S(1)} %dynamic_slice.28, s32[]{:T(128)} %bitcast.25, s32[1]{0:T(128)} %bitcast.36, s32[128]{0:T(128)S(1)} %copy-done, s32[]{:T(128)S(6)} %dynamic_slice.29, s32[1,1]{0,1:T(1,128)} %get-tuple-element.67), kind=kLoop, calls=%fused_computation.116 | loop fusion | flops 7 | bytes 560 | tf_op jit(solution)/shard_map/scatter | solution.py:136
  29.6 2.5 %copy.24 = bf16[128,8192]{0,1:T(8,128)(2,1)} copy(bf16[128,8192]{1,0:T(8,128)(2,1)S(1)} %copy-done.2) | data formatting | bytes 4194304 | tf_op args[0]
  34.1 3.6 %all-to-all-start = ((bf16[128,8,1024]{0,2,1:T(8,128)(2,1)}), bf16[128,8,1024]{0,2,1:T(8,128)(2,1)S(1)}, u32[]{:S(2)}, u32[]{:S(2)}) async-start(bf16[128,8,1024]{0,2,1:T(8,128)(2,1)} %bitcast.21), calls=%async_computation | async-start | bytes 4194304 | tf_op jit(solution)/shard_map/all_to_all | solution.py:162
  38.4 55.8 %all-gather.1 = bf16[128,1,2048]{2,1,0:T(2,128)(2,1)S(1)} all-gather(bf16[1,1,2048]{2,1,0:T(2,128)(2,1)S(1)} %bitcast.237), channel_id=1, replica_groups=mesh['dp'=16,'head'=8] {'dp','head'}, dimensions={0}, use_global_device_ids=true | all-gather | bytes 528384 | tf_op jit(solution)/shard_map/all_gather | solution.py:146
  94.6 2.9 %fusion.27 = bf16[1,4,64,256]{3,0,2,1:T(2,128)(2,1)S(1)} fusion(bf16[16,4,64,256]{3,2,1,0:T(8,128)(2,1)} %bitcast.230, s32[16,1]{0,1:T(1,128)S(1)} %copy-done.5, s32[]{:T(128)S(6)} %axis_index.23), kind=kOutput, calls=%fused_computation.38 | convolution fusion | flops 2097168 | bytes 2228292 | tf_op jit(solution)/shard_map/nk,nabcd->kabcd/dot_general | solution.py:119
  99.5 2.1 %scatter_fusion.1 = bf16[160,64,256]{2,1,0:T(8,128)(2,1)} fusion(bf16[160,64,256]{2,1,0:T(8,128)(2,1)} %scatter_fusion, s32[8]{0:T(128)S(1)} %fusion.62, bf16[8,256]{1,0:T(8,128)(2,1)S(1)} %convolution_convert_fusion.1), kind=kCustom, calls=%fused_computation.6 | custom fusion | bytes 12352 | tf_op jit(solution)/shard_map/scatter | solution.py:157
  101.6 5.3 %gather_fusion.3 = bf16[128,64,256]{2,1,0:T(8,128)(2,1)} fusion(bf16[160,64,256]{2,1,0:T(8,128)(2,1)} %scatter_fusion.1, s32[1024]{0:T(1024)S(1)} %pad_clamp_fusion), kind=kCustom, calls=%fused_computation.3 | custom fusion | bytes 8389120 | tf_op jit(solution)/shard_map/gather | solution.py:160
  106.9 2.6 %scatter_fusion.2 = bf16[160,64,256]{2,1,0:T(8,128)(2,1)} fusion(bf16[160,64,256]{2,1,0:T(8,128)(2,1)} %scatter_fusion.1, s32[16]{0:T(128)S(1)} %fusion.60, bf16[16,64,256]{2,1,0:T(8,128)(2,1)S(1)} %bitcast.231), kind=kCustom, calls=%fused_computation.7 | custom fusion | bytes 1572928 | tf_op jit(solution)/shard_map/scatter | solution.py:172
  109.5 3.1 %gather_fusion.2 = bf16[32,64,256]{2,1,0:T(8,128)(2,1)S(1)} fusion(bf16[160,64,256]{2,1,0:T(8,128)(2,1)} %scatter_fusion.2, s32[1024]{0:T(1024)S(1)} %pad_clamp_fusion.1), kind=kCustom, calls=%fused_computation.2 | custom fusion | bytes 2097280 | tf_op jit(solution)/shard_map/gather | solution.py:173
  112.6 53.5 %while.12 = (s32[]{:T(128)}, bf16[8,128,1024]{1,2,0:T(8,128)(2,1)}, s32[8,128]{1,0:T(8,128)S(1)}, bf16[8,128,1024]{1,2,0:T(8,128)(2,1)S(1)}, bf16[32,1,64,256]{3,2,0,1:T(8,128)(2,1)S(1)}, /*index=5*/s32[]{:T(128)}) while((s32[]{:T(128)}, bf16[8,128,1024]{1,2,0:T(8,128)(2,1)}, s32[8,128]{1,0:T(8,128)S(1)}, bf16[8,128,1024]{1,2,0:T(8,128)(2,1)S(1)}, ...), condition=%wide.region_7.8_spmd, body=%wide.region_4.7_spmd.sunk | while | flops 1101529088 | bytes 28875084 | solution.py:183
  114.5 2.0 fusion.80
  116.5 2.1 %fusion.81 = bf16[128,1,8,128]{0,3,2,1:T(8,128)(2,1)S(1)} fusion(f32[128,8,32,64]{0,3,2,1:T(8,128)S(1)} %get-tuple-element.103, f32[8,128]{1,0:T(8,128)S(1)} %get-tuple-element.104, pred[128,32,64]{0,2,1:T(8,128)(4,1)S(1)} %broadcast_compare_fusion.3, bf16[32,1,64,256]{3,2,0,1:T(8,128)(2,1)S(1)} %get-tuple-element.121, f32[128,8]{0,1:T(8,128)S(1)} %bitcast.234), kind=kOutput, calls=%fused_computation.18.clone.1 | convolution fusion | flops 547618816 | bytes 9445376 | tf_op jit(solution)/shard_map/while/body/eval_jaxpr/kqtmp,mkpd->tkqd/dot_general | solution.py:73
  121.1 2.0 fusion.80
  123.2 2.1 %fusion.81 = bf16[128,1,8,128]{0,3,2,1:T(8,128)(2,1)S(1)} fusion(f32[128,8,32,64]{0,3,2,1:T(8,128)S(1)} %get-tuple-element.103, f32[8,128]{1,0:T(8,128)S(1)} %get-tuple-element.104, pred[128,32,64]{0,2,1:T(8,128)(4,1)S(1)} %broadcast_compare_fusion.3, bf16[32,1,64,256]{3,2,0,1:T(8,128)(2,1)S(1)} %get-tuple-element.121, f32[128,8]{0,1:T(8,128)S(1)} %bitcast.234), kind=kOutput, calls=%fused_computation.18.clone.1 | convolution fusion | flops 547618816 | bytes 9445376 | tf_op jit(solution)/shard_map/while/body/eval_jaxpr/kqtmp,mkpd->tkqd/dot_general | solution.py:73
  127.8 2.0 fusion.80
  129.9 2.1 %fusion.81 = bf16[128,1,8,128]{0,3,2,1:T(8,128)(2,1)S(1)} fusion(f32[128,8,32,64]{0,3,2,1:T(8,128)S(1)} %get-tuple-element.103, f32[8,128]{1,0:T(8,128)S(1)} %get-tuple-element.104, pred[128,32,64]{0,2,1:T(8,128)(4,1)S(1)} %broadcast_compare_fusion.3, bf16[32,1,64,256]{3,2,0,1:T(8,128)(2,1)S(1)} %get-tuple-element.121, f32[128,8]{0,1:T(8,128)S(1)} %bitcast.234), kind=kOutput, calls=%fused_computation.18.clone.1 | convolution fusion | flops 547618816 | bytes 9445376 | tf_op jit(solution)/shard_map/while/body/eval_jaxpr/kqtmp,mkpd->tkqd/dot_general | solution.py:73
  134.5 2.0 fusion.80
  136.5 2.1 %fusion.81 = bf16[128,1,8,128]{0,3,2,1:T(8,128)(2,1)S(1)} fusion(f32[128,8,32,64]{0,3,2,1:T(8,128)S(1)} %get-tuple-element.103, f32[8,128]{1,0:T(8,128)S(1)} %get-tuple-element.104, pred[128,32,64]{0,2,1:T(8,128)(4,1)S(1)} %broadcast_compare_fusion.3, bf16[32,1,64,256]{3,2,0,1:T(8,128)(2,1)S(1)} %get-tuple-element.121, f32[128,8]{0,1:T(8,128)S(1)} %bitcast.234), kind=kOutput, calls=%fused_computation.18.clone.1 | convolution fusion | flops 547618816 | bytes 9445376 | tf_op jit(solution)/shard_map/while/body/eval_jaxpr/kqtmp,mkpd->tkqd/dot_general | solution.py:73
  143.2 2.1 %fusion.81 = bf16[128,1,8,128]{0,3,2,1:T(8,128)(2,1)S(1)} fusion(f32[128,8,32,64]{0,3,2,1:T(8,128)S(1)} %get-tuple-element.103, f32[8,128]{1,0:T(8,128)S(1)} %get-tuple-element.104, pred[128,32,64]{0,2,1:T(8,128)(4,1)S(1)} %broadcast_compare_fusion.3, bf16[32,1,64,256]{3,2,0,1:T(8,128)(2,1)S(1)} %get-tuple-element.121, f32[128,8]{0,1:T(8,128)S(1)} %bitcast.234), kind=kOutput, calls=%fused_computation.18.clone.1 | convolution fusion | flops 547618816 | bytes 9445376 | tf_op jit(solution)/shard_map/while/body/eval_jaxpr/kqtmp,mkpd->tkqd/dot_general | solution.py:73
  149.9 2.1 %fusion.81 = bf16[128,1,8,128]{0,3,2,1:T(8,128)(2,1)S(1)} fusion(f32[128,8,32,64]{0,3,2,1:T(8,128)S(1)} %get-tuple-element.103, f32[8,128]{1,0:T(8,128)S(1)} %get-tuple-element.104, pred[128,32,64]{0,2,1:T(8,128)(4,1)S(1)} %broadcast_compare_fusion.3, bf16[32,1,64,256]{3,2,0,1:T(8,128)(2,1)S(1)} %get-tuple-element.121, f32[128,8]{0,1:T(8,128)S(1)} %bitcast.234), kind=kOutput, calls=%fused_computation.18.clone.1 | convolution fusion | flops 547618816 | bytes 9445376 | tf_op jit(solution)/shard_map/while/body/eval_jaxpr/kqtmp,mkpd->tkqd/dot_general | solution.py:73
  154.6 2.0 fusion.80
  156.6 2.1 %fusion.81 = bf16[128,1,8,128]{0,3,2,1:T(8,128)(2,1)S(1)} fusion(f32[128,8,32,64]{0,3,2,1:T(8,128)S(1)} %get-tuple-element.103, f32[8,128]{1,0:T(8,128)S(1)} %get-tuple-element.104, pred[128,32,64]{0,2,1:T(8,128)(4,1)S(1)} %broadcast_compare_fusion.3, bf16[32,1,64,256]{3,2,0,1:T(8,128)(2,1)S(1)} %get-tuple-element.121, f32[128,8]{0,1:T(8,128)S(1)} %bitcast.234), kind=kOutput, calls=%fused_computation.18.clone.1 | convolution fusion | flops 547618816 | bytes 9445376 | tf_op jit(solution)/shard_map/while/body/eval_jaxpr/kqtmp,mkpd->tkqd/dot_general | solution.py:73
  161.3 2.0 fusion.80
  163.3 2.1 %fusion.81 = bf16[128,1,8,128]{0,3,2,1:T(8,128)(2,1)S(1)} fusion(f32[128,8,32,64]{0,3,2,1:T(8,128)S(1)} %get-tuple-element.103, f32[8,128]{1,0:T(8,128)S(1)} %get-tuple-element.104, pred[128,32,64]{0,2,1:T(8,128)(4,1)S(1)} %broadcast_compare_fusion.3, bf16[32,1,64,256]{3,2,0,1:T(8,128)(2,1)S(1)} %get-tuple-element.121, f32[128,8]{0,1:T(8,128)S(1)} %bitcast.234), kind=kOutput, calls=%fused_computation.18.clone.1 | convolution fusion | flops 547618816 | bytes 9445376 | tf_op jit(solution)/shard_map/while/body/eval_jaxpr/kqtmp,mkpd->tkqd/dot_general | solution.py:73
  166.1 3.9 %all-to-all-start.2 = ((bf16[8,128,1024]{1,2,0:T(8,128)(2,1)}), bf16[8,128,1024]{1,2,0:T(8,128)(2,1)S(1)}, u32[]{:S(2)}, u32[]{:S(2)}) async-start(bf16[8,128,1024]{1,2,0:T(8,128)(2,1)} %get-tuple-element.42), calls=%async_computation.2 | async-start | bytes 4194304 | tf_op jit(solution)/shard_map/all_to_all | solution.py:185
  172.0 3.4 %fusion.65 = (f32[8,8]{1,0:T(8,128)S(1)}, f32[8,8,16,64]{3,1,2,0:T(8,128)S(1)}) fusion(bf16[8,16,1,64,256]{4,3,1,0,2:T(8,128)(2,1)} %bitcast.225, bf16[8,8,128,1]{2,0,1,3:T(8,128)(2,1)S(1)} %fusion.32, pred[8,16,64]{2,1,0:T(8,128)(4,1)S(1)} %broadcast_compare_fusion.1), kind=kOutput, calls=%fused_computation.120 | convolution fusion | flops 16973760 | bytes 2384128 | tf_op jit(solution)/shard_map/skqd,smkpd->skqmp/dot_general | solution.py:22
  175.7 2.2 %fusion.35 = bf16[1,8,8,128]{3,2,1,0:T(8,128)(2,1)S(1)} fusion(bf16[8,16,1,64,256]{4,3,1,0,2:T(8,128)(2,1)} %bitcast.226, f32[8,8,16,64]{3,1,2,0:T(8,128)S(1)} %get-tuple-element.69, f32[8,8]{1,0:T(8,128)S(1)} %get-tuple-element.68, pred[8,16,64]{2,1,0:T(8,128)(4,1)S(1)} %broadcast_compare_fusion.1, f32[8,8]{1,0:T(8,128)S(1)} %fusion.36), kind=kOutput, calls=%fused_computation.48 | convolution fusion | flops 16990208 | bytes 2384384 | tf_op jit(solution)/shard_map/skqmp,smkpd->skqd/dot_general | solution.py:39
  178.4 18.7 %all-to-all-done.2 = bf16[8,128,1024]{1,2,0:T(8,128)(2,1)S(1)} async-done(((bf16[8,128,1024]{1,2,0:T(8,128)(2,1)}), bf16[8,128,1024]{1,2,0:T(8,128)(2,1)S(1)}, u32[]{:S(2)}, u32[]{:S(2)}) %all-to-all-start.2) | async-done | bytes 2097184 | tf_op jit(solution)/shard_map/all_to_all | solution.py:185
  197.2 2.9 %copy.39 = bf16[128,8192]{1,0:T(8,128)(2,1)} copy(bf16[128,8192]{0,1:T(8,128)(2,1)S(1)} %bitcast.227) | data formatting | bytes 4194304 | tf_op jit(solution)/shard_map/all_to_all | solution.py:185
  (121 shorter events, 37.0 us)
Async XLA Ops:
  7.2 22.4 %copy-start.2 = (bf16[128,8192]{1,0:T(8,128)(2,1)S(1)}, bf16[128,8192]{1,0:T(8,128)(2,1)}, u32[]{:S(2)}) copy-start(bf16[128,8192]{1,0:T(8,128)(2,1)} %param.16) | copy-start | bytes 6291460
  7.2 11.0 %copy-start.3 = (bf16[128,2048]{1,0:T(8,128)(2,1)S(1)}, bf16[128,2048]{1,0:T(8,128)(2,1)}, u32[]{:S(2)}) copy-start(bf16[128,2048]{1,0:T(8,128)(2,1)} %param.17) | copy-start | bytes 1572868
  7.2 6.6 %copy-start.1 = (s32[8,16]{1,0:T(8,128)S(1)}, s32[8,16]{1,0:T(8,128)}, u32[]{:S(2)}) copy-start(s32[8,16]{1,0:T(8,128)} %param.21) | copy-start | bytes 1540
  7.2 17.9 %copy-start = (s32[128]{0:T(128)S(1)}, s32[128]{0:T(128)}, u32[]{:S(2)}) copy-start(s32[128]{0:T(128)} %param.23) | copy-start | bytes 1540
  7.2 5.9 %copy-start.6 = (s32[16,1]{0,1:T(1,128)S(1)}, s32[16,1]{0,1:T(1,128)}, u32[]{:S(2)}) copy-start(s32[16,1]{0,1:T(1,128)} %param.25) | copy-start | bytes 196
  7.2 18.7 %copy-start.5 = (s32[16,1]{0,1:T(1,128)S(1)}, s32[16,1]{0,1:T(1,128)}, u32[]{:S(2)}) copy-start(s32[16,1]{0,1:T(1,128)} %param.26) | copy-start | bytes 196
  7.2 87.4 %all-gather.6.cloned.1.call-start = ((), (), s32[]{:S(2)}) async-start(), calls=%async_computation.3 | async-start | bytes 2228224 | tf_op jit(solution)/shard_map/all_gather | solution.py:112
  19.0 18.7 %copy-start.7 = (s32[1,32]{1,0:T(1,128)S(1)}, s32[1,32]{1,0:T(1,128)}, u32[]{:S(2)}) copy-start(s32[1,32]{1,0:T(1,128)} %param.22) | copy-start | bytes 388
  19.0 19.4 %copy-start.4 = (bf16[1,2048]{1,0:T(2,128)(2,1)S(1)}, bf16[1,2048]{1,0:T(2,128)(2,1)}, u32[]{:S(2)}) copy-start(bf16[1,2048]{1,0:T(2,128)(2,1)} %param.19) | copy-start | bytes 12292
  19.0 15.0 %all-to-all-start.1 = ((bf16[128,8,256]{2,0,1:T(8,128)(2,1)}), bf16[128,8,256]{2,0,1:T(8,128)(2,1)S(1)}, u32[]{:S(2)}, u32[]{:S(2)}) async-start(bf16[128,8,256]{2,0,1:T(8,128)(2,1)} %bitcast.188), calls=%async_computation.1 | async-start | bytes 1048576 | tf_op jit(solution)/shard_map/all_to_all | solution.py:163
  23.7 146.5 %all-gather.8.cloned.1.call-start = ((), (), s32[]{:S(2)}) async-start(), calls=%async_computation.4 | async-start | bytes 4227072 | tf_op jit(solution)/shard_map/all_gather | solution.py:140
  25.9 68.5 %copy-start.8 = (s32[128]{0:T(128)S(1)}, s32[128]{0:T(128)}, u32[]{:S(2)}) copy-start(s32[128]{0:T(128)} %param.27) | copy-start | bytes 1540
  34.1 78.5 %all-to-all-start = ((bf16[128,8,1024]{0,2,1:T(8,128)(2,1)}), bf16[128,8,1024]{0,2,1:T(8,128)(2,1)S(1)}, u32[]{:S(2)}, u32[]{:S(2)}) async-start(bf16[128,8,1024]{0,2,1:T(8,128)(2,1)} %bitcast.21), calls=%async_computation | async-start | bytes 4194304 | tf_op jit(solution)/shard_map/all_to_all | solution.py:162
  166.1 31.1 %all-to-all-start.2 = ((bf16[8,128,1024]{1,2,0:T(8,128)(2,1)}), bf16[8,128,1024]{1,2,0:T(8,128)(2,1)S(1)}, u32[]{:S(2)}, u32[]{:S(2)}) async-start(bf16[8,128,1024]{1,2,0:T(8,128)(2,1)} %get-tuple-element.42), calls=%async_computation.2 | async-start | bytes 4194304 | tf_op jit(solution)/shard_map/all_to_all | solution.py:185
Sparse Core Ops, SparseCore 0:
  18.3 47.7 all-gather.5
  69.2 66.0 all-gather.7
where the time goes:
time: 208 us; the launch traced here: 207 us
  blocking collectives  55.8 us (27%)
  local copies, waits for them, and re-layouts  41.3 us (20%)
  matrix products  36.4 us (18%)
  other arithmetic  23.6 us (11%)
  waiting for transfers between devices  21.5 us (10%)
  between operations  15.6 us (8%)
  starting transfers between devices  12.3 us (6%)
    all_gather x1, blocking collectives, per_device(): lax.all_gather(decode_pairs, ('dp', 'head'), axis=0, tiled=True)  55.8 us
    all_to_all x1, waiting for transfers between devices, per_device(): lax.all_to_all(out_span, 'head', split_axis=0, concat_axis=1, tiled=True)  18.7 us
    dot_general x8, matrix products, prefill_block(): jnp.einsum('kqtmp,mkpd->tkqd', weights.astype(jnp.bfloat16), key_pages[.....  16.6 us
    reduce_sum x8, other arithmetic, prefill_block(): weight_sum = jnp.sum(weights, axis=(3, 4))  16.2 us
    dot_general x8, matrix products, prefill_block(): jnp.einsum('tkqd,mkpd->kqtmp', grouped, key_pages[..., :head_size], prefe...  11 us
    unnamed x22, local copies, waits for them, and re-layouts  8.98 us
    dynamic_update_slice x8, local copies, waits for them, and re-layouts, per_device(): outputs = lax.map(attend_block, (blocks, limits))  5.81 us
    gather x1, local copies, waits for them, and re-layouts, per_device(): new_pool[decode_pages]  5.27 us
  transfers between devices with their start and end apart: 5, of which 2 were waited for; matrix products, arithmetic and copies ran while one was open for 42% of the time, Pallas kernels for 0%

commit v1 on v0

v1 whole, which is shorter than its diff:
```python
import jax
import jax.numpy as jnp
from jax import lax
from jax.experimental import pallas as pl
from jax.experimental.pallas import tpu as pltpu
from jax.sharding import PartitionSpec as P

HD = 128
PAGE = 64
MIGP = 4
QPK = 8
NX = 4
LOG2E = 1.4426950408889634
NEG = -1e30
NT = (((1,), (1,)), ((), ()))


def attend_tile(q, k, v, row0, mask_rows):
    keys = k.shape[0]
    scores = lax.dot_general(q, k, NT, preferred_element_type=jnp.float32)
    tail = scores[:, keys - 256 :]
    row = lax.broadcasted_iota(jnp.int32, tail.shape, 0) % mask_rows + row0
    col = lax.broadcasted_iota(jnp.int32, tail.shape, 1)
    tail = jnp.where(col <= row, tail, NEG)
    scores = jnp.concatenate([scores[:, : keys - 256], tail], axis=1)
    top = jnp.max(scores, axis=1, keepdims=True)
    weights = jnp.exp2((scores - top) * (HD**-0.5 * LOG2E)).astype(jnp.bfloat16)
    mixed = jnp.dot(weights, v, preferred_element_type=jnp.float32)
    return mixed[:, :HD] / mixed[:, HD : HD + 1]


def prefill_kernel(table, prefix, q_ref, new_ref, pool_ref, o_ref, pages, keys, values, sem):
    step = pl.program_id(0)
    block = q_ref.shape[0]
    spare = new_ref.shape[0]

    @pl.when(step == 0)
    def _():
        for j in range(16):
            pltpu.make_async_copy(pool_ref.at[table[j], 0], pages.at[j], sem).start()
        new = new_ref[...]
        keys[spare:, :] = new[:, :HD]
        values[spare:, :HD] = new[:, HD:]
        values[spare:, HD:] = jnp.ones((spare, HD), jnp.bfloat16)
        pltpu.make_async_copy(pool_ref.at[pl.ds(0, 16), 0], pages, sem).wait()
        old = pages[...].reshape(16 * PAGE, 2 * HD).astype(jnp.float32)
        seen = lax.broadcasted_iota(jnp.int32, (16 * PAGE, HD), 0) < prefix[0]
        first = new[0:16, :HD].astype(jnp.float32)[0:1, :]
        keys[:spare, :] = jnp.where(seen, old[:, :HD], first).astype(jnp.bfloat16)
        values[:spare, :HD] = jnp.where(seen, old[:, HD:], 0.0).astype(jnp.bfloat16)
        values[:spare, HD:] = jnp.where(seen, 1.0, 0.0).astype(jnp.bfloat16)

    for case in range(spare // 256):

        @pl.when(step // 2 == case)
        def _(case=case):
            used = spare + 256 * (case + 1)
            row0 = (step % 2) * block

            @pl.loop(0, QPK // 2)
            def _(pair):
                c0 = pl.multiple_of(pair * 2 * HD, 2 * HD)
                c1 = pl.multiple_of(pair * 2 * HD + HD, HD)
                q = jnp.concatenate([q_ref[:, pl.ds(c0, HD)], q_ref[:, pl.ds(c1, HD)]], axis=0)
                out = attend_tile(q, keys[:used, :], values[:used, :], row0, block)
                out = out.astype(jnp.bfloat16)
                o_ref[:, pl.ds(c0, HD)] = out[:block]
                o_ref[:, pl.ds(c1, HD)] = out[block:]


def prefill(query_all, pair_all, pool, table, prefix):
    rows, width = query_all.shape
    block = 128
    spec = pl.BlockSpec((block, width), lambda i, t, p: (i, 0))
    return pl.pallas_call(
        prefill_kernel,
        out_shape=jax.ShapeDtypeStruct((rows, width), jnp.bfloat16),
        grid_spec=pltpu.PrefetchScalarGridSpec(
            num_scalar_prefetch=2,
            grid=(rows // block,),
            in_specs=[
                spec,
                pl.BlockSpec((rows, 2 * HD), lambda i, t, p: (0, 0)),
                pl.BlockSpec(memory_space=pl.ANY),
            ],
            out_specs=spec,
            scratch_shapes=[
                pltpu.VMEM((16, PAGE, 2 * HD), jnp.bfloat16),
                pltpu.VMEM((2 * rows, HD), jnp.bfloat16),
                pltpu.VMEM((2 * rows, 2 * HD), jnp.bfloat16),
                pltpu.SemaphoreType.DMA,
            ],
        ),
        compiler_params=pltpu.CompilerParams(
            dimension_semantics=("arbitrary",), vmem_limit_bytes=40 * 1024 * 1024
        ),
        cost_estimate=pl.CostEstimate(
            flops=2 * 8192 * 1600 * 384, bytes_accessed=6 << 20, transcendentals=8192 * 1600
        ),
        name="prefill_attention",
    )(table, prefix, query_all, pair_all, pool)


def decode_kernel(
    dtable, ptable, lengths, scalars, q_ref, pair_ref, mig_ref, new_ref, pool_ref, o_ref, out_ref,
    buf, in_sem, out_sem,
):
    slots = q_ref.shape[0]
    per_slot = buf.shape[1]

    @pl.loop(0, slots * per_slot)
    def _(n):
        s, j = n // per_slot, n % per_slot
        pltpu.make_async_copy(pool_ref.at[dtable[s, j], 0], buf.at[s, j], in_sem.at[s]).start()

    for part in range(2):

        @pl.loop(0, per_slot)
        def _(j, part=part):
            page = ptable[part * per_slot + j]
            pltpu.make_async_copy(
                pool_ref.at[page, 0], buf.at[slots + part, j], in_sem.at[slots + part]
            ).start()

    for s in range(slots):
        pltpu.make_async_copy(pool_ref.at[pl.ds(0, per_slot), 0], buf.at[s], in_sem.at[s]).wait()

        @pl.when(scalars[0] == s)
        def _(s=s):
            buf[s, 0:MIGP] = mig_ref[...]

        length = lengths[s]
        page, row = length // PAGE, length % PAGE
        base = pl.multiple_of((row // 16) * 16, 16)
        tile = buf[s, page, pl.ds(base, 16), :].astype(jnp.float32)
        hit = lax.broadcasted_iota(jnp.int32, tile.shape, 0) == row - base
        tile = jnp.where(hit, pair_ref[s : s + 1, :], tile)
        buf[s, page, pl.ds(base, 16), :] = tile.astype(jnp.bfloat16)

        @pl.loop(0, per_slot)
        def _(j, s=s):
            pltpu.make_async_copy(buf.at[s, j], out_ref.at[dtable[s, j], 0], out_sem.at[s]).start()

        kv = buf[s].reshape(per_slot * PAGE, 2 * HD)
        scores = lax.dot_general(q_ref[s], kv[:, :HD], NT, preferred_element_type=jnp.float32)
        seen = lax.broadcasted_iota(jnp.int32, scores.shape, 1) <= length
        scores = jnp.where(seen, scores, NEG)
        top = jnp.max(scores, axis=1, keepdims=True)
        weights = jnp.exp2((scores - top) * (HD**-0.5 * LOG2E))
        total = jnp.sum(weights, axis=1, keepdims=True)
        mixed = jnp.dot(weights.astype(jnp.bfloat16), kv[:, HD:], preferred_element_type=jnp.float32)
        o_ref[s] = (mixed / total).astype(jnp.bfloat16)

    first = scalars[1]
    for part in range(2):
        at = slots + part
        pltpu.make_async_copy(pool_ref.at[pl.ds(0, per_slot), 0], buf.at[at], in_sem.at[at]).wait()

        @pl.loop(0, per_slot)
        def _(j, part=part, at=at):
            logical = part * per_slot + j
            page = ptable[logical]
            fresh = jnp.logical_and(logical >= first, logical < first + 16)

            @pl.when(fresh)
            def _():
                pltpu.make_async_copy(
                    new_ref.at[logical - first], out_ref.at[page, 0], out_sem.at[at]
                ).start()

            @pl.when(jnp.logical_not(fresh))
            def _():
                pltpu.make_async_copy(buf.at[at, j], out_ref.at[page, 0], out_sem.at[at]).start()

    for at in range(slots + 2):
        pltpu.make_async_copy(buf.at[at], out_ref.at[pl.ds(0, per_slot), 0], out_sem.at[at]).wait()


def decode_and_store(query, pairs, arriving, pair_all, pool, dtable, ptable, lengths, scalars):
    slots, per_slot = dtable.shape
    vmem = pl.BlockSpec(memory_space=pltpu.VMEM)
    smem = pl.BlockSpec(memory_space=pltpu.SMEM)
    hbm = pl.BlockSpec(memory_space=pl.ANY)
    return pl.pallas_call(
        decode_kernel,
        out_shape=(
            jax.ShapeDtypeStruct(query.shape, jnp.bfloat16),
            jax.ShapeDtypeStruct(pool.shape, pool.dtype),
        ),
        in_specs=[smem] * 4 + [vmem] * 4 + [hbm],
        out_specs=(vmem, hbm),
        scratch_shapes=[
            pltpu.VMEM((slots + 2, per_slot, PAGE, 2 * HD), jnp.bfloat16),
            pltpu.SemaphoreType.DMA((slots + 2,)),
            pltpu.SemaphoreType.DMA((slots + 2,)),
        ],
        compiler_params=pltpu.CompilerParams(vmem_limit_bytes=24 * 1024 * 1024),
        cost_estimate=pl.CostEstimate(
            flops=2 * 64 * 1024 * 256, bytes_accessed=11 << 20, transcendentals=64 * 1024
        ),
        name="decode_and_pool",
    )(dtable, ptable, lengths, scalars, query, pairs, arriving, pair_all, pool)


def per_device(
    prefill_query,
    prefill_pairs,
    decode_query,
    decode_pairs,
    cache_pool,
    decode_pages,
    prefill_pages,
    cache_length,
    prefix_length,
    migrant_slot,
    migrant_target,
    arrivals,
):
    my_group = lax.axis_index("dp")
    my_z, my_x = my_group // NX, my_group % NX
    heads = lax.axis_size("head")
    groups = lax.axis_size("dp")
    nz = groups // NX
    slot_count = decode_pages.shape[0]
    along_x = [[z * NX + x for x in range(NX)] for z in range(nz)]
    along_z = [[z * NX + x for z in range(nz)] for x in range(NX)]

    tokens = jnp.concatenate(
        [decode_query.reshape(1, heads, QPK * HD), decode_pairs.reshape(1, heads, 2 * HD)], axis=2
    )
    tokens = lax.all_to_all(tokens, "head", split_axis=1, concat_axis=0, tiled=True)
    width = tokens.shape[2]
    pair_all = lax.all_to_all(prefill_pairs, "head", split_axis=1, concat_axis=0, tiled=True)
    query_all = lax.all_to_all(prefill_query, "head", split_axis=1, concat_axis=0, tiled=True)

    my_slot = migrant_slot[my_group, 0]
    own_pages = lax.dynamic_slice_in_dim(decode_pages, my_slot, 1)[0, :MIGP]
    leaving = cache_pool[own_pages]
    page_size = leaving.size
    parcel = jnp.concatenate([leaving.reshape(-1, 2 * HD), tokens.reshape(-1, 2 * HD)])
    page_rows = page_size // (2 * HD)
    row = lax.all_to_all(
        jnp.broadcast_to(parcel[None], (NX,) + parcel.shape),
        "dp", split_axis=0, concat_axis=0, tiled=True, axis_index_groups=along_x,
    )
    target = migrant_target[:, 0]
    row_target = lax.dynamic_slice_in_dim(target, my_z * NX, NX)
    want = jnp.arange(nz, dtype=jnp.int32) * NX + my_x
    pick = jnp.argmax((row_target[None, :] == want[:, None]).astype(jnp.int32), axis=1)
    chosen_pages = row[:, :page_rows][pick]
    row_tokens = row[:, page_rows:].reshape(NX * slot_count, width)
    row_slots = lax.dynamic_slice_in_dim(arrivals, my_z * NX * slot_count, NX * slot_count)
    want_slots = (want[:, None] * slot_count + jnp.arange(slot_count, dtype=jnp.int32)).reshape(-1)
    onehot = (want_slots[:, None] == row_slots[None, :]).astype(jnp.bfloat16)
    sorted_tokens = jnp.dot(onehot, row_tokens, preferred_element_type=jnp.float32)
    sorted_tokens = sorted_tokens.astype(jnp.bfloat16).reshape(nz, -1, 2 * HD)
    column = lax.all_to_all(
        jnp.concatenate([chosen_pages, sorted_tokens], axis=1),
        "dp", split_axis=0, concat_axis=0, tiled=True, axis_index_groups=along_z,
    )
    source = jnp.argmax((target == my_group).astype(jnp.int32)).astype(jnp.int32)
    arriving = lax.dynamic_index_in_dim(column[:, :page_rows], source // NX, keepdims=False)
    arriving = arriving.reshape(MIGP, PAGE, 2 * HD)
    my_tokens = jnp.sum(column[:, page_rows:].astype(jnp.float32), axis=0).reshape(slot_count, width)
    query_rows = my_tokens[:, : QPK * HD].astype(jnp.bfloat16).reshape(slot_count, QPK, HD)
    pair_rows = my_tokens[:, QPK * HD :]

    incoming = cache_length[source * slot_count + migrant_slot[source, 0]]
    own_len = lax.dynamic_slice_in_dim(cache_length, my_group * slot_count, slot_count)
    lengths = jnp.where(jnp.arange(slot_count, dtype=jnp.int32) == my_slot, incoming, own_len)

    table = prefill_pages[0]
    out_span = prefill(query_all, pair_all, cache_pool, table, prefix_length)
    prefill_attended = lax.all_to_all(out_span, "head", split_axis=0, concat_axis=1, tiled=True)
    scalars = jnp.stack([my_slot, prefix_length[0] // PAGE])
    decoded, new_pool = decode_and_store(
        query_rows, pair_rows, arriving, pair_all.reshape(-1, PAGE, 2 * HD), cache_pool,
        decode_pages, table, lengths, scalars,
    )
    return (prefill_attended, decoded.reshape(slot_count, -1), new_pool)


def solution(mesh):
    placed = (
        P(("dp", "head"), None),
        P(("dp", "head"), None),
        P(("dp", "head"), None),
        P(("dp", "head"), None),
        P("dp", "head", None, None),
        P("dp", None),
        P("dp", None),
        P(),
        P("dp"),
        P(),
        P(),
        P(),
    )
    return jax.shard_map(
        per_device,
        mesh=mesh,
        in_specs=placed,
        out_specs=(P(("dp", "head"), None), P("dp", "head"), P("dp", "head", None, None)),
        check_vma=False,
    )
```

time: 208 us -> 165 us (0.79)
  Pallas kernels: 0 us -> 57.8 us
  blocking collectives: 55.8 us -> 0 us
  matrix products: 36.4 us -> 0.21 us
  waiting for transfers between devices: 21.5 us -> 40.5 us
  local copies, waits for them, and re-layouts: 41.3 us -> 22.9 us
  other arithmetic: 23.6 us -> 6.58 us
  starting transfers between devices: 12.3 us -> 27.2 us
  between operations: 15.6 us -> 8.36 us
    pallas_call x0 -> x2, Pallas kernels: none -> 57.8 us  [the longest x1 42.7 us: prefill(): pl.pallas_call(prefill_kernel, out_shape=jax.ShapeDtypeStruct((rows, widt...]
    all_gather x1 -> x0, blocking collectives: 55.8 us -> none  [per_device(): lax.all_gather(decode_pairs, ('dp', 'head'), axis=0, tiled=True)]
    dot_general x21 -> x1, matrix products: 36.4 us -> 0.21 us  [per_device(): jnp.dot(onehot, row_tokens, preferred_element_type=jnp.float32)]
    all_to_all x1, waiting for transfers between devices: 0.01 us -> 21.7 us  [per_device(): lax.all_to_all(prefill_query, 'head', split_axis=1, concat_axis=0, tiled=...]
    reduce_sum x10 -> x1, other arithmetic: 17.2 us -> 0.01 us  [per_device(): jnp.sum(column[:, page_rows:].astype(jnp.float32), axis=0)]
    all_to_all x1, waiting for transfers between devices: 18.7 us -> 3.1 us  [per_device(): lax.all_to_all(out_span, 'head', split_axis=0, concat_axis=1, tiled=True)]
    all_to_all x0 -> x3, starting transfers between devices: none -> 14.2 us  [the longest x1 5.31 us: per_device(): lax.all_to_all(jnp.concatenate([chosen_pages, sorted_tokens], axis=1), 'd...]
    gather x5 -> x1, local copies, waits for them, and re-layouts: 10.3 us -> 1.62 us  [per_device(): chosen_pages = row[:, :page_rows][pick]]
  transfers between devices with their start and end apart: 5 -> 6, of which waited for: 2 -> 4; matrix products, arithmetic and copies ran while one was open for 42% -> 11% of each run, Pallas kernels for 0% -> 35%
where the time goes in v1:
time: 165 us; the launch traced here: 164 us
  Pallas kernels  57.8 us (35%)
  waiting for transfers between devices  40.5 us (25%)
  starting transfers between devices  27.2 us (16%)
  local copies, waits for them, and re-layouts  22.9 us (14%)
  between operations  8.36 us (5%)
  other arithmetic  6.58 us (4%)
    pallas_call x1, Pallas kernels, prefill(): pl.pallas_call(prefill_kernel, out_shape=jax.ShapeDtypeStruct((rows, widt...  42.7 us
    all_to_all x1, waiting for transfers between devices, per_device(): lax.all_to_all(prefill_query, 'head', split_axis=1, concat_axis=0, tiled=...  21.7 us
    pallas_call x1, Pallas kernels, decode_and_store(): pl.pallas_call(decode_kernel, out_shape=(jax.ShapeDtypeStruct(query.shape...  15.1 us
    all_to_all x1, waiting for transfers between devices, per_device(): lax.all_to_all(jnp.broadcast_to(parcel[None], (NX,) + parcel.shape), 'dp'...  8.63 us
    all_to_all x1, waiting for transfers between devices, per_device(): lax.all_to_all(prefill_pairs, 'head', split_axis=1, concat_axis=0, tiled=...  7.07 us
    unnamed x20, local copies, waits for them, and re-layouts  6.76 us
    all_to_all x1, starting transfers between devices, per_device(): lax.all_to_all(jnp.concatenate([chosen_pages, sorted_tokens], axis=1), 'd...  5.31 us
    all_to_all x1, starting transfers between devices, per_device(): lax.all_to_all(prefill_pairs, 'head', split_axis=1, concat_axis=0, tiled=...  4.94 us
  transfers between devices with their start and end apart: 6, of which 4 were waited for; matrix products, arithmetic and copies ran while one was open for 11% of the time, Pallas kernels for 35%

profile of v1, /device:TPU:0, one launch (start us, length us, event | category | flops | bytes accessed | tf_op | source)
XLA Modules:
  0.0 163.5 jit_solution(16948909461483376755)
XLA Ops:
  0.6 0.8 fusion.8
  2.0 0.8 reduce.40
  2.7 0.6 reshape.147
  3.4 4.6 %all-to-all-start.3 = ((bf16[8,2,640]{2,1,0:T(2,128)(2,1)}), bf16[8,2,640]{2,1,0:T(2,128)(2,1)S(1)}, u32[]{:S(2)}, u32[]{:S(2)}) async-start(bf16[8,2,640]{2,1,0:T(2,128)(2,1)} %reshape.147), calls=%async_computation.3 | async-start | bytes 40960 | tf_op jit(solution)/shard_map/all_to_all | solution.py:231
  7.9 1.3 fusion.6
  11.1 1.4 constant_dynamic-slice_fusion.4
  14.3 0.7 constant_dynamic-slice_fusion.2
  15.0 1.9 %copy.39 = bf16[16,8,8,256]{3,2,0,1:T(8,128)(2,1)} copy(bf16[16,8,8,256]{3,2,1,0:T(8,128)(2,1)} %bitcast.69) | data formatting | bytes 1048576 | tf_op jit(solution)/shard_map/all_to_all | solution.py:233
  16.8 4.9 %all-to-all-start.1 = ((bf16[128,8,256]{2,0,1:T(8,128)(2,1)}), bf16[128,8,256]{2,0,1:T(8,128)(2,1)S(1)}, u32[]{:S(2)}, u32[]{:S(2)}) async-start(bf16[128,8,256]{2,0,1:T(8,128)(2,1)} %bitcast.51), calls=%async_computation.1 | async-start | bytes 1048576 | tf_op jit(solution)/shard_map/all_to_all | solution.py:233
  21.8 3.0 %gather_fusion = bf16[4,64,256]{2,1,0:T(8,128)(2,1)S(1)} fusion(bf16[160,64,256]{2,1,0:T(8,128)(2,1)} %bitcast.57, s32[1024]{0:T(1024)S(1)} %pad_clamp_fusion.1), kind=kCustom, calls=%fused_computation | custom fusion | bytes 262160 | tf_op jit(solution)/shard_map/gather | solution.py:238
  25.0 7.1 %all-to-all-done.1 = bf16[128,8,256]{2,0,1:T(8,128)(2,1)S(1)} async-done(((bf16[128,8,256]{2,0,1:T(8,128)(2,1)}), bf16[128,8,256]{2,0,1:T(8,128)(2,1)S(1)}, u32[]{:S(2)}, u32[]{:S(2)}) %all-to-all-start.1) | async-done | bytes 524320 | tf_op jit(solution)/shard_map/all_to_all | solution.py:233
  32.1 0.9 broadcast_in_dim.8
  33.0 4.3 %all-to-all-start.4 = ((bf16[4,296,256]{2,1,0:T(8,128)(2,1)}), bf16[4,296,256]{2,1,0:T(8,128)(2,1)S(1)}, u32[]{:S(2)}, u32[]{:S(2)}) async-start(bf16[4,296,256]{2,1,0:T(8,128)(2,1)} %broadcast_in_dim.8), calls=%async_computation.4 | async-start | bytes 1212416 | tf_op jit(solution)/shard_map/all_to_all | solution.py:242
  37.3 1.5 copy.38
  38.8 8.6 %all-to-all-done.4 = bf16[4,296,256]{2,1,0:T(8,128)(2,1)S(1)} async-done(((bf16[4,296,256]{2,1,0:T(8,128)(2,1)}), bf16[4,296,256]{2,1,0:T(8,128)(2,1)S(1)}, u32[]{:S(2)}, u32[]{:S(2)}) %all-to-all-start.4) | async-done | bytes 606240 | tf_op jit(solution)/shard_map/all_to_all | solution.py:242
  47.4 3.7 %all-to-all-start = ((bf16[128,8,1024]{2,0,1:T(8,128)(2,1)}), bf16[128,8,1024]{2,0,1:T(8,128)(2,1)S(1)}, u32[]{:S(2)}, u32[]{:S(2)}) async-start(bf16[128,8,1024]{2,0,1:T(8,128)(2,1)} %bitcast.65), calls=%async_computation | async-start | bytes 4194304 | tf_op jit(solution)/shard_map/all_to_all | solution.py:234
  52.2 0.7 iota_reduce_fusion
  53.3 0.8 slice.33
  54.1 1.6 gather_fusion.1
  55.7 0.9 pad_maximum_fusion
  56.6 21.7 %all-to-all-done = bf16[128,8,1024]{2,0,1:T(8,128)(2,1)S(1)} async-done(((bf16[128,8,1024]{2,0,1:T(8,128)(2,1)}), bf16[128,8,1024]{2,0,1:T(8,128)(2,1)S(1)}, u32[]{:S(2)}, u32[]{:S(2)}) %all-to-all-start) | async-done | bytes 2097184 | tf_op jit(solution)/shard_map/all_to_all | solution.py:234
  78.3 5.3 %all-to-all-start.5 = ((bf16[4,296,256]{2,1,0:T(8,128)(2,1)}), bf16[4,296,256]{2,1,0:T(8,128)(2,1)S(1)}, u32[]{:S(2)}, u32[]{:S(2)}) async-start(bf16[4,296,256]{2,1,0:T(8,128)(2,1)} %pad_maximum_fusion), calls=%async_computation.5 | async-start | bytes 1212416 | tf_op jit(solution)/shard_map/all_to_all | solution.py:257
  83.6 2.5 %copy-done = bf16[160,1,64,256]{3,2,1,0:T(8,128)(2,1)S(1)} copy-done((bf16[160,1,64,256]{3,2,1,0:T(8,128)(2,1)S(1)}, bf16[160,1,64,256]{3,2,1,0:T(8,128)(2,1)}, u32[]{:S(2)}) %copy-start) | copy-done | bytes 5242904
  86.1 42.7 %prefill_attention.1 = bf16[1024,1024]{1,0:T(8,128)(2,1)} custom-call(s32[32]{0:T(128)S(1)} %bitcast.63, s32[1]{0:T(128)} %copy.41.prefix, bf16[1024,1024]{1,0:T(8,128)(2,1)S(1)} %bitcast.60, bf16[1024,256]{1,0:T(8,128)(2,1)S(1)} %bitcast.58, bf16[160,1,64,256]{3,2,1,0:T(8,128)(2,1)S(1)} %copy-done), custom_call_target="tpu_custom_call" | custom-call | flops 10066329600 | bytes 6291456 | tf_op jit(solution)/shard_map/prefill_attention/pallas_call | solution.py:75
  128.8 4.4 %all-to-all-start.2 = ((bf16[8,128,1024]{2,1,0:T(8,128)(2,1)}), bf16[8,128,1024]{2,1,0:T(8,128)(2,1)}, u32[]{:S(2)}, u32[]{:S(2)}) async-start(bf16[8,128,1024]{2,1,0:T(8,128)(2,1)} %bitcast.5), calls=%async_computation.2 | async-start | bytes 4194304 | tf_op jit(solution)/shard_map/all_to_all | solution.py:274
  136.9 1.3 compare_select_fusion.2.lengths
  138.3 0.7 pad_add_fusion.scalars
  139.1 2.5 %copy-done.1 = bf16[160,1,64,256]{3,2,1,0:T(8,128)(2,1)S(1)} copy-done((bf16[160,1,64,256]{3,2,1,0:T(8,128)(2,1)S(1)}, bf16[160,1,64,256]{3,2,1,0:T(8,128)(2,1)}, u32[]{:S(2)}) %copy-start.1) | copy-done | bytes 5242904
  141.6 15.1 %decode_and_pool.1 = (bf16[8,8,128]{2,1,0:T(8,128)(2,1)S(1)}, bf16[160,1,64,256]{3,2,1,0:T(8,128)(2,1)}) custom-call(s32[8,16]{1,0:T(8,128)S(1)} %copy-done.2, s32[32]{0:T(128)S(1)} %bitcast.64, s32[8]{0:T(128)S(1)} %compare_select_fusion.2.lengths, s32[2]{0:T(128)S(1)} %pad_add_fusion.scalars, bf16[8,8,128]{2,1,0:T(8,128)(2,1)S(1)} %copy.30.q_ref, ...), custom_call_target="tpu_custom_call" | custom-call | flops 33554432 | bytes 11534336 | tf_op jit(solution)/shard_map/decode_and_pool/pallas_call | solution.py:184
  156.7 0.6 copy.40
  157.3 3.1 %all-to-all-done.2 = bf16[8,128,1024]{2,1,0:T(8,128)(2,1)} async-done(((bf16[8,128,1024]{2,1,0:T(8,128)(2,1)}), bf16[8,128,1024]{2,1,0:T(8,128)(2,1)}, u32[]{:S(2)}, u32[]{:S(2)}) %all-to-all-start.2) | async-done | bytes 2097184 | tf_op jit(solution)/shard_map/all_to_all | solution.py:274
  160.4 3.1 %copy.33 = bf16[8,16,8,1024]{3,2,0,1:T(8,128)(2,1)} copy(bf16[8,16,8,1024]{3,2,1,0:T(8,128)(2,1)} %bitcast.31) | data formatting | bytes 4194304 | tf_op jit(solution)/shard_map/all_to_all | solution.py:274
  (42 shorter events, 2.1 us)
Async XLA Ops:
  3.4 13.5 %all-to-all-start.3 = ((bf16[8,2,640]{2,1,0:T(2,128)(2,1)}), bf16[8,2,640]{2,1,0:T(2,128)(2,1)S(1)}, u32[]{:S(2)}, u32[]{:S(2)}) async-start(bf16[8,2,640]{2,1,0:T(2,128)(2,1)} %reshape.147), calls=%async_computation.3 | async-start | bytes 40960 | tf_op jit(solution)/shard_map/all_to_all | solution.py:231
  16.8 20.4 %copy-start.4 = (bf16[128,8192]{1,0:T(8,128)(2,1)S(1)}, bf16[128,8192]{1,0:T(8,128)(2,1)}, u32[]{:S(2)}) copy-start(bf16[128,8192]{1,0:T(8,128)(2,1)} %param.12) | copy-start | bytes 6291460
  16.8 15.3 %all-to-all-start.1 = ((bf16[128,8,256]{2,0,1:T(8,128)(2,1)}), bf16[128,8,256]{2,0,1:T(8,128)(2,1)S(1)}, u32[]{:S(2)}, u32[]{:S(2)}) async-start(bf16[128,8,256]{2,0,1:T(8,128)(2,1)} %bitcast.51), calls=%async_computation.1 | async-start | bytes 1048576 | tf_op jit(solution)/shard_map/all_to_all | solution.py:233
  33.0 14.5 %all-to-all-start.4 = ((bf16[4,296,256]{2,1,0:T(8,128)(2,1)}), bf16[4,296,256]{2,1,0:T(8,128)(2,1)S(1)}, u32[]{:S(2)}, u32[]{:S(2)}) async-start(bf16[4,296,256]{2,1,0:T(8,128)(2,1)} %broadcast_in_dim.8), calls=%async_computation.4 | async-start | bytes 1212416 | tf_op jit(solution)/shard_map/all_to_all | solution.py:242
  47.4 4.6 %copy-start.7 = (s32[128]{0:T(128)S(1)}, s32[128]{0:T(128)}, u32[]{:S(2)}) copy-start(s32[128]{0:T(128)} %param.23) | copy-start | bytes 1540
  47.4 4.7 %copy-start.6 = (s32[16,1]{0,1:T(1,128)S(1)}, s32[16,1]{0,1:T(1,128)}, u32[]{:S(2)}) copy-start(s32[16,1]{0,1:T(1,128)} %param.22) | copy-start | bytes 196
  47.4 30.9 %all-to-all-start = ((bf16[128,8,1024]{2,0,1:T(8,128)(2,1)}), bf16[128,8,1024]{2,0,1:T(8,128)(2,1)S(1)}, u32[]{:S(2)}, u32[]{:S(2)}) async-start(bf16[128,8,1024]{2,0,1:T(8,128)(2,1)} %bitcast.65), calls=%async_computation | async-start | bytes 4194304 | tf_op jit(solution)/shard_map/all_to_all | solution.py:234
  53.3 30.3 %copy-start.3 = (s32[1,32]{1,0:T(1,128)S(1)}, s32[1,32]{1,0:T(1,128)}, u32[]{:S(2)}) copy-start(s32[1,32]{1,0:T(1,128)} %param.18) | copy-start | bytes 388
  78.3 50.5 %all-to-all-start.5 = ((bf16[4,296,256]{2,1,0:T(8,128)(2,1)}), bf16[4,296,256]{2,1,0:T(8,128)(2,1)S(1)}, u32[]{:S(2)}, u32[]{:S(2)}) async-start(bf16[4,296,256]{2,1,0:T(8,128)(2,1)} %pad_maximum_fusion), calls=%async_computation.5 | async-start | bytes 1212416 | tf_op jit(solution)/shard_map/all_to_all | solution.py:257
  83.6 2.5 %copy-start = (bf16[160,1,64,256]{3,2,1,0:T(8,128)(2,1)S(1)}, bf16[160,1,64,256]{3,2,1,0:T(8,128)(2,1)}, u32[]{:S(2)}) copy-start(bf16[160,1,64,256]{3,2,1,0:T(8,128)(2,1)} %pool_ref.3) | copy-start | bytes 15728644
  128.8 7.5 %copy-start.5 = (s32[128]{0:T(128)S(1)}, s32[128]{0:T(128)}, u32[]{:S(2)}) copy-start(s32[128]{0:T(128)} %param.19) | copy-start | bytes 1540
  128.8 10.3 %copy-start.2 = (s32[8,16]{1,0:T(8,128)S(1)}, s32[8,16]{1,0:T(8,128)}, u32[]{:S(2)}) copy-start(s32[8,16]{1,0:T(8,128)} %dtable.1) | copy-start | bytes 1540
  128.8 31.6 %all-to-all-start.2 = ((bf16[8,128,1024]{2,1,0:T(8,128)(2,1)}), bf16[8,128,1024]{2,1,0:T(8,128)(2,1)}, u32[]{:S(2)}, u32[]{:S(2)}) async-start(bf16[8,128,1024]{2,1,0:T(8,128)(2,1)} %bitcast.5), calls=%async_computation.2 | async-start | bytes 4194304 | tf_op jit(solution)/shard_map/all_to_all | solution.py:274
  139.1 2.5 %copy-start.1 = (bf16[160,1,64,256]{3,2,1,0:T(8,128)(2,1)S(1)}, bf16[160,1,64,256]{3,2,1,0:T(8,128)(2,1)}, u32[]{:S(2)}) copy-start(bf16[160,1,64,256]{3,2,1,0:T(8,128)(2,1)} %pool_ref.3) | copy-start | bytes 15728644

commit v2 on v1

v2 whole, which is shorter than its diff:
```python
import jax
import jax.numpy as jnp
from jax import lax
from jax.experimental import pallas as pl
from jax.experimental.pallas import tpu as pltpu
from jax.sharding import PartitionSpec as P

HD = 128
PAGE = 64
MIGP = 4
QPK = 8
LOG2E = 1.4426950408889634
NEG = -1e30
NT = (((1,), (1,)), ((), ()))


def attend_tile(q, k, v, row0, mask_rows):
    keys = k.shape[0]
    scores = lax.dot_general(q, k, NT, preferred_element_type=jnp.float32)
    tail = scores[:, keys - 256 :]
    row = lax.broadcasted_iota(jnp.int32, tail.shape, 0) % mask_rows + row0
    col = lax.broadcasted_iota(jnp.int32, tail.shape, 1)
    tail = jnp.where(col <= row, tail, NEG)
    scores = jnp.concatenate([scores[:, : keys - 256], tail], axis=1)
    top = jnp.max(scores, axis=1, keepdims=True)
    weights = jnp.exp2((scores - top) * (HD**-0.5 * LOG2E)).astype(jnp.bfloat16)
    mixed = jnp.dot(weights, v, preferred_element_type=jnp.float32)
    return mixed[:, :HD] / mixed[:, HD : HD + 1]


def prefill_kernel(
    prefix, q_ref, pair_ref, tok_ref, leave_ref, old_ref,
    out_ref, pair_out, tok_out, mig_out,
    qbuf, pbuf, tbuf, obuf, keys, values,
    q_send, q_recv, p_send, p_recv, t_send, t_recv, o_send, o_recv,
    a_send, a_recv, m_send, m_recv,
):
    heads, block, width = qbuf.shape
    groups = mig_out.shape[0]
    spare = heads * block
    d = lax.axis_index("dp")
    h = lax.axis_index("head")
    chip, core = h // 2, h % 2
    chips = heads // 2

    def head_at(step, sign):
        ring = step // 2
        ring = ring + ring // 2 - 2 * (ring // 3)
        return ((chip + sign * ring + chips) % chips) * 2 + (core + step) % 2

    def cols(p, n):
        return pl.ds(pl.multiple_of(p * n, n), n)

    def to_head(src, dst, send, recv, p):
        return pltpu.make_async_remote_copy(
            src_ref=src, dst_ref=dst, send_sem=send.at[p], recv_sem=recv.at[h],
            device_id=(d, p), device_id_type=pl.DeviceIdType.MESH,
        )

    def to_group(src, dst, send, recv, g):
        return pltpu.make_async_remote_copy(
            src_ref=src, dst_ref=dst, send_sem=send.at[g], recv_sem=recv.at[d],
            device_id=(g, h), device_id_type=pl.DeviceIdType.MESH,
        )

    def landed(ref, sem):
        pltpu.make_async_copy(ref, ref, sem).wait()

    barrier = pltpu.get_barrier_semaphore()

    @pl.loop(1, heads)
    def _(k):
        pl.semaphore_signal(
            barrier, inc=1, device_id=(d, (h + k) % heads), device_id_type=pl.DeviceIdType.MESH
        )

    @pl.loop(1, groups)
    def _(k):
        pl.semaphore_signal(
            barrier, inc=1, device_id=((d + k) % groups, h), device_id_type=pl.DeviceIdType.MESH
        )

    pl.semaphore_wait(barrier, heads + groups - 2)

    pltpu.make_async_copy(tok_ref.at[h], tbuf.at[d, h], t_recv.at[h]).start()
    pltpu.make_async_copy(pair_ref.at[:, cols(h, 2 * HD)], pbuf.at[h], p_recv.at[h]).start()
    pltpu.make_async_copy(q_ref.at[:, cols(h, width)], qbuf.at[h], q_recv.at[h]).start()
    pltpu.make_async_copy(leave_ref, mig_out.at[d], m_recv.at[d]).start()

    @pl.loop(1, heads)
    def _(k):
        p = head_at(k, 1)
        to_head(tok_ref.at[p], tbuf.at[d, h], t_send, t_recv, p).start()
        to_head(pair_ref.at[:, cols(p, 2 * HD)], pbuf.at[h], p_send, p_recv, p).start()

    @pl.loop(1, heads)
    def _(k):
        p = head_at(k, 1)
        to_head(q_ref.at[:, cols(p, width)], qbuf.at[h], q_send, q_recv, p).start()

    @pl.loop(1, groups)
    def _(k):
        g = (d + k) % groups
        to_group(leave_ref, mig_out.at[d], m_send, m_recv, g).start()

    @pl.loop(0, heads)
    def _(p):
        landed(tbuf.at[d, p], t_recv.at[p])

    @pl.loop(1, groups)
    def _(k):
        g = (d + k) % groups
        to_group(tbuf.at[d], tbuf.at[d], a_send, a_recv, g).start()

    @pl.loop(0, heads)
    def _(p):
        landed(pbuf.at[p], p_recv.at[p])

    new = pbuf[...].reshape(spare, 2 * HD)
    pair_out[...] = new
    keys[spare:, :] = new[:, :HD]
    values[spare:, :HD] = new[:, HD:]
    values[spare:, HD:] = jnp.ones((spare, HD), jnp.bfloat16)
    old = old_ref[...].astype(jnp.float32)
    seen = lax.broadcasted_iota(jnp.int32, (spare, HD), 0) < prefix[0]
    first = new[0:16, :HD].astype(jnp.float32)[0:1, :]
    keys[:spare, :] = jnp.where(seen, old[:, :HD], first).astype(jnp.bfloat16)
    values[:spare, :HD] = jnp.where(seen, old[:, HD:], 0.0).astype(jnp.bfloat16)
    values[:spare, HD:] = jnp.where(seen, 1.0, 0.0).astype(jnp.bfloat16)

    @pl.loop(0, heads)
    def _(step):
        src = head_at(step, -1)
        landed(qbuf.at[src], q_recv.at[src])
        for case in range(spare // 256):

            @pl.when(src // 2 == case)
            def _(case=case):
                used = spare + 256 * (case + 1)
                row0 = (src % 2) * block

                @pl.loop(0, QPK // 2)
                def _(pair):
                    c0 = pl.multiple_of(pair * 2 * HD, 2 * HD)
                    c1 = pl.multiple_of(pair * 2 * HD + HD, HD)
                    q = jnp.concatenate(
                        [qbuf[src, :, pl.ds(c0, HD)], qbuf[src, :, pl.ds(c1, HD)]], axis=0
                    )
                    out = attend_tile(q, keys[:used, :], values[:used, :], row0, block)
                    out = out.astype(jnp.bfloat16)
                    obuf[src, :, pl.ds(c0, HD)] = out[:block]
                    obuf[src, :, pl.ds(c1, HD)] = out[block:]

        @pl.when(step == 0)
        def _():
            pltpu.make_async_copy(obuf.at[h], out_ref.at[:, cols(h, width)], o_recv.at[h]).start()

        @pl.when(step > 0)
        def _():
            to_head(obuf.at[src], out_ref.at[:, cols(h, width)], o_send, o_recv, src).start()

    @pl.loop(1, groups)
    def _(k):
        g = (d + k) % groups
        landed(tbuf.at[g], a_recv.at[g])
        landed(tbuf.at[d], a_send.at[g])
        landed(mig_out.at[g], m_recv.at[g])
        landed(leave_ref, m_send.at[g])

    landed(mig_out.at[d], m_recv.at[d])
    tok_out[...] = tbuf[...]

    @pl.loop(1, heads)
    def _(k):
        p = (h + k) % heads
        landed(tok_ref.at[p], t_send.at[p])
        landed(pbuf.at[p], p_send.at[p])
        landed(qbuf.at[p], q_send.at[p])
        landed(obuf.at[p], o_send.at[p])

    @pl.loop(0, heads)
    def _(p):
        landed(out_ref.at[:, cols(p, width)], o_recv.at[p])


def prefill(prefix, query, pairs, tokens, leaving, old, heads, groups):
    block, columns = query.shape
    width = columns // heads
    rows = block * heads
    bf16 = jnp.bfloat16
    vmem = pl.BlockSpec(memory_space=pltpu.VMEM)
    hbm = pl.BlockSpec(memory_space=pl.ANY)
    sem = pltpu.SemaphoreType.DMA
    return pl.pallas_call(
        prefill_kernel,
        out_shape=(
            jax.ShapeDtypeStruct((block, columns), bf16),
            jax.ShapeDtypeStruct((rows, 2 * HD), bf16),
            jax.ShapeDtypeStruct((groups,) + tokens.shape, bf16),
            jax.ShapeDtypeStruct((groups,) + leaving.shape, bf16),
        ),
        in_specs=[pl.BlockSpec(memory_space=pltpu.SMEM), hbm, hbm, vmem, vmem, vmem],
        out_specs=(hbm, vmem, vmem, hbm),
        scratch_shapes=[
            pltpu.VMEM((heads, block, width), bf16),
            pltpu.VMEM((heads, block, 2 * HD), bf16),
            pltpu.VMEM((groups,) + tokens.shape, bf16),
            pltpu.VMEM((heads, block, width), bf16),
            pltpu.VMEM((2 * rows, HD), bf16),
            pltpu.VMEM((2 * rows, 2 * HD), bf16),
        ]
        + [sem((heads,))] * 8
        + [sem((groups,))] * 4,
        compiler_params=pltpu.CompilerParams(
            collective_id=0, has_side_effects=True, vmem_limit_bytes=44 * 1024 * 1024
        ),
        name="prefill_exchange",
    )(prefix, query, pairs, tokens, leaving, old)


def decode_kernel(
    dtable, ptable, lengths, scalars, q_ref, pair_ref, mig_ref, new_ref, pool_ref, o_ref, out_ref,
    buf, in_sem, out_sem,
):
    slots = q_ref.shape[0]
    per_slot = buf.shape[1]

    @pl.loop(0, slots * per_slot)
    def _(n):
        s, j = n // per_slot, n % per_slot
        pltpu.make_async_copy(pool_ref.at[dtable[s, j], 0], buf.at[s, j], in_sem.at[s]).start()

    for part in range(2):

        @pl.loop(0, per_slot)
        def _(j, part=part):
            page = ptable[part * per_slot + j]
            pltpu.make_async_copy(
                pool_ref.at[page, 0], buf.at[slots + part, j], in_sem.at[slots + part]
            ).start()

    for s in range(slots):
        pltpu.make_async_copy(pool_ref.at[pl.ds(0, per_slot), 0], buf.at[s], in_sem.at[s]).wait()

        @pl.when(scalars[0] == s)
        def _(s=s):
            buf[s, 0:MIGP] = mig_ref[...]

        length = lengths[s]
        page, row = length // PAGE, length % PAGE
        base = pl.multiple_of((row // 16) * 16, 16)
        tile = buf[s, page, pl.ds(base, 16), :].astype(jnp.float32)
        hit = lax.broadcasted_iota(jnp.int32, tile.shape, 0) == row - base
        tile = jnp.where(hit, pair_ref[s : s + 1, :], tile)
        buf[s, page, pl.ds(base, 16), :] = tile.astype(jnp.bfloat16)

        @pl.loop(0, per_slot)
        def _(j, s=s):
            pltpu.make_async_copy(buf.at[s, j], out_ref.at[dtable[s, j], 0], out_sem.at[s]).start()

        kv = buf[s].reshape(per_slot * PAGE, 2 * HD)
        scores = lax.dot_general(q_ref[s], kv[:, :HD], NT, preferred_element_type=jnp.float32)
        seen = lax.broadcasted_iota(jnp.int32, scores.shape, 1) <= length
        scores = jnp.where(seen, scores, NEG)
        top = jnp.max(scores, axis=1, keepdims=True)
        weights = jnp.exp2((scores - top) * (HD**-0.5 * LOG2E))
        total = jnp.sum(weights, axis=1, keepdims=True)
        mixed = jnp.dot(weights.astype(jnp.bfloat16), kv[:, HD:], preferred_element_type=jnp.float32)
        o_ref[s] = (mixed / total).astype(jnp.bfloat16)

    first = scalars[1]
    for part in range(2):
        at = slots + part
        pltpu.make_async_copy(pool_ref.at[pl.ds(0, per_slot), 0], buf.at[at], in_sem.at[at]).wait()

        @pl.loop(0, per_slot)
        def _(j, part=part, at=at):
            logical = part * per_slot + j
            page = ptable[logical]
            fresh = jnp.logical_and(logical >= first, logical < first + 16)

            @pl.when(fresh)
            def _():
                pltpu.make_async_copy(
                    new_ref.at[logical - first], out_ref.at[page, 0], out_sem.at[at]
                ).start()

            @pl.when(jnp.logical_not(fresh))
            def _():
                pltpu.make_async_copy(buf.at[at, j], out_ref.at[page, 0], out_sem.at[at]).start()

    for at in range(slots + 2):
        pltpu.make_async_copy(buf.at[at], out_ref.at[pl.ds(0, per_slot), 0], out_sem.at[at]).wait()


def decode_and_store(query, pairs, arriving, pair_all, pool, dtable, ptable, lengths, scalars):
    slots, per_slot = dtable.shape
    vmem = pl.BlockSpec(memory_space=pltpu.VMEM)
    smem = pl.BlockSpec(memory_space=pltpu.SMEM)
    hbm = pl.BlockSpec(memory_space=pl.ANY)
    return pl.pallas_call(
        decode_kernel,
        out_shape=(
            jax.ShapeDtypeStruct(query.shape, jnp.bfloat16),
            jax.ShapeDtypeStruct(pool.shape, pool.dtype),
        ),
        in_specs=[smem] * 4 + [vmem] * 4 + [hbm],
        out_specs=(vmem, hbm),
        scratch_shapes=[
            pltpu.VMEM((slots + 2, per_slot, PAGE, 2 * HD), jnp.bfloat16),
            pltpu.SemaphoreType.DMA((slots + 2,)),
            pltpu.SemaphoreType.DMA((slots + 2,)),
        ],
        compiler_params=pltpu.CompilerParams(vmem_limit_bytes=24 * 1024 * 1024),
        cost_estimate=pl.CostEstimate(
            flops=2 * 64 * 1024 * 256, bytes_accessed=11 << 20, transcendentals=64 * 1024
        ),
        name="decode_and_pool",
    )(dtable, ptable, lengths, scalars, query, pairs, arriving, pair_all, pool)


def per_device(
    prefill_query,
    prefill_pairs,
    decode_query,
    decode_pairs,
    cache_pool,
    decode_pages,
    prefill_pages,
    cache_length,
    prefix_length,
    migrant_slot,
    migrant_target,
    arrivals,
):
    my_group = lax.axis_index("dp")
    heads = lax.axis_size("head")
    groups = lax.axis_size("dp")
    slot_count = decode_pages.shape[0]

    my_slot = migrant_slot[my_group, 0]
    own_pages = lax.dynamic_slice_in_dim(decode_pages, my_slot, 1)[0, :MIGP]
    table = prefill_pages[0]
    picked = cache_pool[jnp.concatenate([own_pages, table[: 1024 // PAGE]]), 0]
    leaving = picked[:MIGP].reshape(-1, 2 * HD)
    old = picked[MIGP:].reshape(-1, 2 * HD)
    tokens = jnp.concatenate(
        [
            decode_query.reshape(heads, QPK, HD),
            decode_pairs.reshape(heads, 2, HD),
            jnp.zeros((heads, 6, HD), jnp.bfloat16),
        ],
        axis=1,
    )
    prefill_attended, pair_all, all_tokens, all_leaving = prefill(
        prefix_length, prefill_query, prefill_pairs, tokens, leaving, old, heads, groups
    )

    source = jnp.argmax((migrant_target[:, 0] == my_group).astype(jnp.int32)).astype(jnp.int32)
    arriving = lax.dynamic_index_in_dim(all_leaving, source, keepdims=False)
    arriving = arriving.reshape(MIGP, PAGE, 2 * HD)
    wanted = my_group * slot_count + jnp.arange(slot_count, dtype=jnp.int32)
    onehot = (wanted[:, None] == arrivals[None, :]).astype(jnp.bfloat16)
    my_tokens = jnp.dot(
        onehot, all_tokens.reshape(groups * slot_count, -1), preferred_element_type=jnp.float32
    )
    query_rows = my_tokens[:, : QPK * HD].astype(jnp.bfloat16).reshape(slot_count, QPK, HD)
    pair_rows = my_tokens[:, QPK * HD : (QPK + 2) * HD]

    incoming = cache_length[source * slot_count + migrant_slot[source, 0]]
    own_len = lax.dynamic_slice_in_dim(cache_length, my_group * slot_count, slot_count)
    lengths = jnp.where(jnp.arange(slot_count, dtype=jnp.int32) == my_slot, incoming, own_len)

    scalars = jnp.stack([my_slot, prefix_length[0] // PAGE])
    decoded, new_pool = decode_and_store(
        query_rows, pair_rows, arriving, pair_all.reshape(-1, PAGE, 2 * HD), cache_pool,
        decode_pages, table, lengths, scalars,
    )
    return (prefill_attended, decoded.reshape(slot_count, -1), new_pool)


def solution(mesh):
    placed = (
        P(("dp", "head"), None),
        P(("dp", "head"), None),
        P(("dp", "head"), None),
        P(("dp", "head"), None),
        P("dp", "head", None, None),
        P("dp", None),
        P("dp", None),
        P(),
        P("dp"),
        P(),
        P(),
        P(),
    )
    return jax.shard_map(
        per_device,
        mesh=mesh,
        in_specs=placed,
        out_specs=(P(("dp", "head"), None), P("dp", "head"), P("dp", "head", None, None)),
        check_vma=False,
    )
```

time: 165 us -> 110 us (0.67)
  waiting for transfers between devices: 40.5 us -> 0 us
  Pallas kernels: 57.8 us -> 86.3 us
  starting transfers between devices: 27.2 us -> 0 us
  local copies, waits for them, and re-layouts: 22.9 us -> 10.8 us
  between operations: 8.36 us -> 6.69 us
    all_to_all x6 -> x0, waiting for transfers between devices: 40.5 us -> none  [the longest x1 21.7 us: per_device(): lax.all_to_all(prefill_query, 'head', split_axis=1, concat_axis=0, tiled=...]
    pallas_call x1, Pallas kernels: 42.7 us -> 71.2 us  [prefill(): pl.pallas_call(prefill_kernel, out_shape=(jax.ShapeDtypeStruct((block, co...]
    all_to_all x6 -> x0, starting transfers between devices: 27.2 us -> none  [the longest x1 5.31 us: per_device(): lax.all_to_all(jnp.concatenate([chosen_pages, sorted_tokens], axis=1), 'd...]
    all_to_all x4 -> x0, local copies, waits for them, and re-layouts: 6.65 us -> none  [the longest x1 3.15 us: per_device(): lax.all_to_all(out_span, 'head', split_axis=0, concat_axis=1, tiled=True)]
    unnamed x20 -> x16, local copies, waits for them, and re-layouts: 6.76 us -> 3.7 us
    dynamic_slice x1 -> x2, local copies, waits for them, and re-layouts: 0.59 us -> 2.57 us  [per_device(): incoming = cache_length[source * slot_count + migrant_slot[source, 0]]]
    gather x2 -> x1, local copies, waits for them, and re-layouts: 4.66 us -> 3.08 us  [per_device(): picked = cache_pool[jnp.concatenate([own_pages, table[:1024 // PAGE]]), 0]]
  transfers between devices with their start and end apart: 6 -> 0, of which waited for: 4 -> 0; matrix products, arithmetic and copies ran while one was open for 11% -> 0% of each run, Pallas kernels for 35% -> 0%
where the time goes in v2:
time: 110 us
  Pallas kernels  86.3 us (78%)
  local copies, waits for them, and re-layouts  10.8 us (10%)
  between operations  6.69 us (6%)
  other arithmetic  5.79 us (5%)
    pallas_call x1, Pallas kernels, prefill(): pl.pallas_call(prefill_kernel, out_shape=(jax.ShapeDtypeStruct((block, co...  71.2 us
    pallas_call x1, Pallas kernels, decode_and_store(): pl.pallas_call(decode_kernel, out_shape=(jax.ShapeDtypeStruct(query.shape...  15.1 us
    unnamed x16, local copies, waits for them, and re-layouts  3.7 us
    gather x1, local copies, waits for them, and re-layouts, per_device(): picked = cache_pool[jnp.concatenate([own_pages, table[:1024 // PAGE]]), 0]  3.08 us
    dynamic_slice x2, local copies, waits for them, and re-layouts, per_device(): incoming = cache_length[source * slot_count + migrant_slot[source, 0]]  2.57 us

profile of v2, /device:TPU:0, one launch (start us, length us, event | category | flops | bytes accessed | tf_op | source)
XLA Modules:
  0.0 109.9 jit_solution(8527627173817521193)
XLA Ops:
  0.6 0.0 copy-start.2
  1.4 0.7 slice_bitcast_fusion
  2.0 0.1 pad.7.clone
  2.1 1.3 %fusion.8 = (s32[]{:T(128)}, s32[]{:T(128)}) fusion(s32[16,1]{0,1:T(1,128)} %param.22, s32[]{:T(128)S(6)} %axis_index.15), kind=kLoop, calls=%fused_computation.20 | loop fusion | flops 137 | bytes 76 | tf_op jit(solution)/shard_map/per_device/reduce | solution.py:359
  6.0 1.3 %constant_dynamic-slice_fusion = (s32[1,1]{0,1:T(1,128)}, s32[1,1]{0,1:T(1,128)}) fusion(s32[16,1]{0,1:T(1,128)} %param.21, s32[]{:T(128)S(6)} %select_n.43, s32[]{:T(128)S(6)} %select_n.40), kind=kLoop, calls=%fused_computation.15 | loop fusion | bytes 24 | tf_op jit(solution)/shard_map/dynamic_slice | solution.py:370
  9.9 1.2 %dynamic_slice.22 = s32[1]{0:T(128)} dynamic-slice(s32[128]{0:T(128)} %param.19, s32[]{:T(128)S(6)} %select_n.44), dynamic_slice_sizes={1} | dynamic-slice | bytes 12 | tf_op jit(solution)/shard_map/dynamic_slice | solution.py:370
  11.2 2.0 %compare_select_fusion.1.lengths = s32[8]{0:T(128)S(1)} fusion(s32[128]{0:T(128)} %param.19, s32[]{:T(128)S(6)} %select_n.45, s32[]{:T(128)} %bitcast.9, s32[]{:T(128)} %bitcast), kind=kLoop, calls=%fused_computation.14 | loop fusion | flops 16 | bytes 76 | tf_op jit(solution)/shard_map/jit(_where)/select_n | solution.py:372
  13.2 0.7 constant_dynamic-slice_fusion.2
  13.9 0.1 fusion.11
  14.0 0.7 pad_add_fusion.scalars
  14.7 0.7 reduce.19
  15.4 0.8 reduce.18
  16.3 0.1 maximum_maximum_fusion.tok_ref
  16.4 3.1 %gather_fusion = bf16[20,64,256]{2,1,0:T(8,128)(2,1)S(1)} fusion(bf16[160,1,64,256]{3,2,1,0:T(8,128)(2,1)} %pool_ref.1, s32[20]{0:T(128)S(1)} %fusion.11), kind=kCustom, calls=%fused_computation | custom fusion | bytes 1310880 | tf_op jit(solution)/shard_map/gather | solution.py:344
  19.4 0.0 copy-start.5
  19.5 0.0 copy-start
  19.5 0.0 copy-done.2
  19.5 0.0 copy-start.1
  19.6 1.7 %copy-done.1 = bf16[128,8192]{1,0:T(8,128)(2,1)S(1)} copy-done((bf16[128,8192]{1,0:T(8,128)(2,1)S(1)}, bf16[128,8192]{1,0:T(8,128)(2,1)}, u32[]{:S(2)}) %copy-start.1) | copy-done | bytes 2097176
  21.3 0.0 copy-start.3
  21.3 0.0 copy-start.4
  21.3 71.2 %prefill_exchange.1 = (bf16[128,8192]{1,0:T(8,128)(2,1)S(1)}, bf16[1024,256]{1,0:T(8,128)(2,1)S(1)}, bf16[16,8,16,128]{3,2,1,0:T(8,128)(2,1)S(1)}, bf16[16,256,256]{2,1,0:T(8,128)(2,1)S(1)}) custom-call(s32[1]{0:T(128)} %copy.27.prefix, bf16[128,8192]{1,0:T(8,128)(2,1)S(1)} %copy-done.1, bf16[128,2048]{1,0:T(8,128)(2,1)S(1)} %copy-done.2, ...), custom_call_target="tpu_custom_call" | custom-call | tf_op jit(solution)/shard_map/prefill_exchange/pallas_call | solution.py:194
  92.5 0.0 copy-done.5
  92.5 0.2 fusion
  92.8 0.0 copy-done
  92.8 0.0 copy-done.3
  92.8 0.0 copy-done.4
  92.8 15.1 %decode_and_pool.1 = (bf16[8,8,128]{2,1,0:T(8,128)(2,1)S(1)}, bf16[160,1,64,256]{3,2,1,0:T(8,128)(2,1)}) custom-call(s32[8,16]{1,0:T(8,128)S(1)} %copy-done.3, s32[32]{0:T(128)S(1)} %bitcast.47, s32[8]{0:T(128)S(1)} %compare_select_fusion.1.lengths, s32[2]{0:T(128)S(1)} %pad_add_fusion.scalars, bf16[8,8,128]{2,1,0:T(8,128)(2,1)S(1)} %bitcast.45, ...), custom_call_target="tpu_custom_call" | custom-call | flops 33554432 | bytes 11534336 | tf_op jit(solution)/shard_map/decode_and_pool/pallas_call | solution.py:301
  108.0 0.6 copy.24
  108.6 1.3 %copy.28 = bf16[128,8192]{1,0:T(8,128)(2,1)} copy(bf16[128,8192]{1,0:T(8,128)(2,1)S(1)} %get-tuple-element.22) | data formatting | bytes 4194304
  (9 shorter events, 0.1 us)
Async XLA Ops:
  0.6 18.9 %copy-start.2 = (bf16[128,2048]{1,0:T(8,128)(2,1)S(1)}, bf16[128,2048]{1,0:T(8,128)(2,1)}, u32[]{:S(2)}) copy-start(bf16[128,2048]{1,0:T(8,128)(2,1)} %pair_ref.1) | copy-start | bytes 1572868
  19.4 73.1 %copy-start.5 = (s32[128]{0:T(128)S(1)}, s32[128]{0:T(128)}, u32[]{:S(2)}) copy-start(s32[128]{0:T(128)} %param.23) | copy-start | bytes 1540
  19.5 73.3 %copy-start = (bf16[160,1,64,256]{3,2,1,0:T(8,128)(2,1)S(1)}, bf16[160,1,64,256]{3,2,1,0:T(8,128)(2,1)}, u32[]{:S(2)}) copy-start(bf16[160,1,64,256]{3,2,1,0:T(8,128)(2,1)} %pool_ref.1) | copy-start | bytes 15728644
  19.5 1.7 %copy-start.1 = (bf16[128,8192]{1,0:T(8,128)(2,1)S(1)}, bf16[128,8192]{1,0:T(8,128)(2,1)}, u32[]{:S(2)}) copy-start(bf16[128,8192]{1,0:T(8,128)(2,1)} %q_ref.1) | copy-start | bytes 6291460
  21.3 71.5 %copy-start.3 = (s32[8,16]{1,0:T(8,128)S(1)}, s32[8,16]{1,0:T(8,128)}, u32[]{:S(2)}) copy-start(s32[8,16]{1,0:T(8,128)} %dtable.1) | copy-start | bytes 1540
  21.3 71.5 %copy-start.4 = (s32[1,32]{1,0:T(1,128)S(1)}, s32[1,32]{1,0:T(1,128)}, u32[]{:S(2)}) copy-start(s32[1,32]{1,0:T(1,128)} %param.18) | copy-start | bytes 388

commit v3 on v2

--- a/solution.py
+++ b/solution.py
@@ -218,40 +218,89 @@
     )(prefix, query, pairs, tokens, leaving, old)
 
 
+def gather_kernel(where, dtable, ptable, migrant, pool_ref, leave_ref, old_ref, sem):
+    slot = migrant[where[0], 0]
+    for j in range(leave_ref.shape[0]):
+        pltpu.make_async_copy(pool_ref.at[dtable[slot, j], 0], leave_ref.at[j], sem.at[0]).start()
+    for j in range(old_ref.shape[0]):
+        pltpu.make_async_copy(pool_ref.at[ptable[0, j], 0], old_ref.at[j], sem.at[1]).start()
+    for k, ref in enumerate((leave_ref, old_ref)):
+        pltpu.make_async_copy(pool_ref.at[pl.ds(0, ref.shape[0]), 0], ref, sem.at[k]).wait()
+
+
+def gather(where, dtable, ptable, migrant, pool, prefix_pages):
+    vmem = pl.BlockSpec(memory_space=pltpu.VMEM)
+    smem = pl.BlockSpec(memory_space=pltpu.SMEM)
+    return pl.pallas_call(
+        gather_kernel,
+        out_shape=tuple(
+            jax.ShapeDtypeStruct((n, PAGE, 2 * HD), pool.dtype) for n in (MIGP, prefix_pages)
+        ),
+        in_specs=[smem] * 4 + [pl.BlockSpec(memory_space=pl.ANY)],
+        out_specs=(vmem, vmem),
+        scratch_shapes=[pltpu.SemaphoreType.DMA((2,))],
+        name="gather_pages",
+    )(where, dtable, ptable, migrant, pool)
+
+
 def decode_kernel(
-    dtable, ptable, lengths, scalars, q_ref, pair_ref, mig_ref, new_ref, pool_ref, o_ref, out_ref,
-    buf, in_sem, out_sem,
+    where, dtable, ptable, cached, migrant, target, prefix, arrivals,
+    tok_ref, mig_ref, new_ref, pool_ref, o_ref, out_ref,
+    buf, rows, in_sem, out_sem,
 ):
-    slots = q_ref.shape[0]
+    slots = o_ref.shape[0]
     per_slot = buf.shape[1]
+    group = where[0]
+    my_slot = migrant[group, 0]
+    source = lax.fori_loop(
+        0, target.shape[0], lambda i, found: jnp.where(target[i, 0] == group, i, found), 0
+    )
+    incoming = cached[source * slots + migrant[source, 0]]
 
     @pl.loop(0, slots * per_slot)
     def _(n):
         s, j = n // per_slot, n % per_slot
-        pltpu.make_async_copy(pool_ref.at[dtable[s, j], 0], buf.at[s, j], in_sem.at[s]).start()
+        moved = jnp.logical_and(s == my_slot, j < MIGP)
+
+        @pl.when(moved)
+        def _():
+            pltpu.make_async_copy(
+                mig_ref.at[source, jnp.minimum(j, MIGP - 1)], buf.at[s, j], in_sem.at[s]
+            ).start()
+
+        @pl.when(jnp.logical_not(moved))
+        def _():
+            pltpu.make_async_copy(pool_ref.at[dtable[s, j], 0], buf.at[s, j], in_sem.at[s]).start()
 
     for part in range(2):
 
         @pl.loop(0, per_slot)
         def _(j, part=part):
-            page = ptable[part * per_slot + j]
+            page = ptable[0, part * per_slot + j]
             pltpu.make_async_copy(
                 pool_ref.at[page, 0], buf.at[slots + part, j], in_sem.at[slots + part]
             ).start()
 
+    @pl.loop(0, arrivals.shape[0])
+    def _(i):
+        slot = arrivals[i]
+
+        @pl.when(slot // slots == group)
+        def _():
+            rows[slot % slots] = i
+
     for s in range(slots):
         pltpu.make_async_copy(pool_ref.at[pl.ds(0, per_slot), 0], buf.at[s], in_sem.at[s]).wait()
 
-        @pl.when(scalars[0] == s)
-        def _(s=s):
-            buf[s, 0:MIGP] = mig_ref[...]
-
-        length = lengths[s]
+        token = tok_ref[rows[s]]
+        wide = token.astype(jnp.float32)
+        pair = jnp.concatenate([wide[QPK : QPK + 1], wide[QPK + 1 : QPK + 2]], axis=1)
+        length = jnp.where(my_slot == s, incoming, cached[group * slots + s])
         page, row = length // PAGE, length % PAGE
         base = pl.multiple_of((row // 16) * 16, 16)
         tile = buf[s, page, pl.ds(base, 16), :].astype(jnp.float32)
         hit = lax.broadcasted_iota(jnp.int32, tile.shape, 0) == row - base
-        tile = jnp.where(hit, pair_ref[s : s + 1, :], tile)
+        tile = jnp.where(hit, pair, tile)
         buf[s, page, pl.ds(base, 16), :] = tile.astype(jnp.bfloat16)
 
         @pl.loop(0, per_slot)
@@ -259,16 +308,16 @@
             pltpu.make_async_copy(buf.at[s, j], out_ref.at[dtable[s, j], 0], out_sem.at[s]).start()
 
         kv = buf[s].reshape(per_slot * PAGE, 2 * HD)
-        scores = lax.dot_general(q_ref[s], kv[:, :HD], NT, preferred_element_type=jnp.float32)
+        scores = lax.dot_general(token, kv[:, :HD], NT, preferred_element_type=jnp.float32)
         seen = lax.broadcasted_iota(jnp.int32, scores.shape, 1) <= length
         scores = jnp.where(seen, scores, NEG)
         top = jnp.max(scores, axis=1, keepdims=True)
         weights = jnp.exp2((scores - top) * (HD**-0.5 * LOG2E))
         total = jnp.sum(weights, axis=1, keepdims=True)
         mixed = jnp.dot(weights.astype(jnp.bfloat16), kv[:, HD:], preferred_element_type=jnp.float32)
-        o_ref[s] = (mixed / total).astype(jnp.bfloat16)
-
-    first = scalars[1]
+        o_ref[s] = (mixed / total)[:QPK].astype(jnp.bfloat16)
+
+    first = prefix[0] // PAGE
     for part in range(2):
         at = slots + part
         pltpu.make_async_copy(pool_ref.at[pl.ds(0, per_slot), 0], buf.at[at], in_sem.at[at]).wait()
@@ -276,7 +325,7 @@
         @pl.loop(0, per_slot)
         def _(j, part=part, at=at):
             logical = part * per_slot + j
-            page = ptable[logical]
+            page = ptable[0, logical]
             fresh = jnp.logical_and(logical >= first, logical < first + 16)
 
             @pl.when(fresh)
@@ -293,7 +342,9 @@
         pltpu.make_async_copy(buf.at[at], out_ref.at[pl.ds(0, per_slot), 0], out_sem.at[at]).wait()
 
 
-def decode_and_store(query, pairs, arriving, pair_all, pool, dtable, ptable, lengths, scalars):
+def decode_and_store(
+    where, dtable, ptable, cached, migrant, target, prefix, arrivals, tokens, moved, pair_all, pool
+):
     slots, per_slot = dtable.shape
     vmem = pl.BlockSpec(memory_space=pltpu.VMEM)
     smem = pl.BlockSpec(memory_space=pltpu.SMEM)
@@ -301,13 +352,14 @@
     return pl.pallas_call(
         decode_kernel,
         out_shape=(
-            jax.ShapeDtypeStruct(query.shape, jnp.bfloat16),
+            jax.ShapeDtypeStruct((slots, QPK, HD), jnp.bfloat16),
             jax.ShapeDtypeStruct(pool.shape, pool.dtype),
         ),
-        in_specs=[smem] * 4 + [vmem] * 4 + [hbm],
+        in_specs=[smem] * 8 + [vmem, hbm, vmem, hbm],
         out_specs=(vmem, hbm),
         scratch_shapes=[
             pltpu.VMEM((slots + 2, per_slot, PAGE, 2 * HD), jnp.bfloat16),
+            pltpu.SMEM((slots,), jnp.int32),
             pltpu.SemaphoreType.DMA((slots + 2,)),
             pltpu.SemaphoreType.DMA((slots + 2,)),
         ],
@@ -316,7 +368,10 @@
             flops=2 * 64 * 1024 * 256, bytes_accessed=11 << 20, transcendentals=64 * 1024
         ),
         name="decode_and_pool",
-    )(dtable, ptable, lengths, scalars, query, pairs, arriving, pair_all, pool)
+    )(
+        where, dtable, ptable, cached, migrant, target, prefix, arrivals, tokens, moved, pair_all,
+        pool,
+    )
 
 
 def per_device(
@@ -333,17 +388,17 @@
     migrant_target,
     arrivals,
 ):
-    my_group = lax.axis_index("dp")
+    where = lax.axis_index("dp").astype(jnp.int32).reshape(1)
     heads = lax.axis_size("head")
     groups = lax.axis_size("dp")
     slot_count = decode_pages.shape[0]
-
-    my_slot = migrant_slot[my_group, 0]
-    own_pages = lax.dynamic_slice_in_dim(decode_pages, my_slot, 1)[0, :MIGP]
-    table = prefill_pages[0]
-    picked = cache_pool[jnp.concatenate([own_pages, table[: 1024 // PAGE]]), 0]
-    leaving = picked[:MIGP].reshape(-1, 2 * HD)
-    old = picked[MIGP:].reshape(-1, 2 * HD)
+    prefix_pages = prefill_pages.shape[1] // 2
+
+    leaving, old = gather(
+        where, decode_pages, prefill_pages, migrant_slot, cache_pool, prefix_pages
+    )
+    leaving = leaving.reshape(-1, 2 * HD)
+    old = old.reshape(-1, 2 * HD)
     tokens = jnp.concatenate(
         [
             decode_query.reshape(heads, QPK, HD),
@@ -356,25 +411,11 @@
         prefix_length, prefill_query, prefill_pairs, tokens, leaving, old, heads, groups
     )
 
-    source = jnp.argmax((migrant_target[:, 0] == my_group).astype(jnp.int32)).astype(jnp.int32)
-    arriving = lax.dynamic_index_in_dim(all_leaving, source, keepdims=False)
-    arriving = arriving.reshape(MIGP, PAGE, 2 * HD)
-    wanted = my_group * slot_count + jnp.arange(slot_count, dtype=jnp.int32)
-    onehot = (wanted[:, None] == arrivals[None, :]).astype(jnp.bfloat16)
-    my_tokens = jnp.dot(
-        onehot, all_tokens.reshape(groups * slot_count, -1), preferred_element_type=jnp.float32
-    )
-    query_rows = my_tokens[:, : QPK * HD].astype(jnp.bfloat16).reshape(slot_count, QPK, HD)
-    pair_rows = my_tokens[:, QPK * HD : (QPK + 2) * HD]
-
-    incoming = cache_length[source * slot_count + migrant_slot[source, 0]]
-    own_len = lax.dynamic_slice_in_dim(cache_length, my_group * slot_count, slot_count)
-    lengths = jnp.where(jnp.arange(slot_count, dtype=jnp.int32) == my_slot, incoming, own_len)
-
-    scalars = jnp.stack([my_slot, prefix_length[0] // PAGE])
     decoded, new_pool = decode_and_store(
-        query_rows, pair_rows, arriving, pair_all.reshape(-1, PAGE, 2 * HD), cache_pool,
-        decode_pages, table, lengths, scalars,
+        where, decode_pages, prefill_pages, cache_length, migrant_slot, migrant_target,
+        prefix_length, arrivals, all_tokens.reshape(groups * slot_count, -1, HD),
+        all_leaving.reshape(groups, MIGP, PAGE, 2 * HD), pair_all.reshape(-1, PAGE, 2 * HD),
+        cache_pool,
     )
     return (prefill_attended, decoded.reshape(slot_count, -1), new_pool)
 

time: 110 us -> 105 us (0.955)
  Pallas kernels: 86.3 us -> 92.6 us
  between operations: 6.69 us -> 1.43 us
  other arithmetic: 5.79 us -> 1.65 us
  local copies, waits for them, and re-layouts: 10.8 us -> 8.53 us
    pallas_call x1 -> x2, Pallas kernels: 15.1 us -> 21.4 us  [the longest x1 18.5 us: decode_and_store(): pl.pallas_call(decode_kernel, out_shape=(jax.ShapeDtypeStruct((slots, QPK...]
    unnamed x16 -> x24, local copies, waits for them, and re-layouts: 3.7 us -> 8.45 us
    dynamic_slice x4 -> x0, local copies, waits for them, and re-layouts: 3.27 us -> none  [the longest x2 2.57 us: per_device(): incoming = cache_length[source * slot_count + migrant_slot[source, 0]]]
    gather x1 -> x0, local copies, waits for them, and re-layouts: 3.08 us -> none  [per_device(): picked = cache_pool[jnp.concatenate([own_pages, table[:1024 // PAGE]]), 0]]
    another operation x2 -> x0, other arithmetic: 2.02 us -> none  [the longest x1 1.31 us: per_device(): jnp.argmax((migrant_target[:, 0] == my_group).astype(jnp.int32))]
    select_n x1 -> x0, other arithmetic: 2.02 us -> none  [per_device(): jnp.where(jnp.arange(slot_count, dtype=jnp.int32) == my_slot, incoming, o...]
where the time goes in v3:
time: 105 us; the launch traced here: 104 us
  Pallas kernels  92.6 us (88%)
  local copies, waits for them, and re-layouts  8.53 us (8%)
  other arithmetic  1.65 us (2%)
  between operations  1.43 us (1%)
    pallas_call x1, Pallas kernels, prefill(): pl.pallas_call(prefill_kernel, out_shape=(jax.ShapeDtypeStruct((block, co...  71.2 us
    pallas_call x1, Pallas kernels, decode_and_store(): pl.pallas_call(decode_kernel, out_shape=(jax.ShapeDtypeStruct((slots, QPK...  18.5 us
    unnamed x24, local copies, waits for them, and re-layouts  8.45 us
    pallas_call x1, Pallas kernels, gather(): pl.pallas_call(gather_kernel, out_shape=tuple((jax.ShapeDtypeStruct((n, P...  2.91 us

profile of v3, /device:TPU:0, one launch (start us, length us, event | category | flops | bytes accessed | tf_op | source)
XLA Modules:
  0.0 104.2 jit_solution(15727639371637814613)
XLA Ops:
  1.3 0.1 pad.2.clone
  1.4 0.7 reduce.1
  2.1 1.3 %copy.15.migrant = s32[16,1]{1,0:T(8,128)} copy(s32[16,1]{0,1:T(1,128)} %param.21) | data formatting | bytes 128 | tf_op args[9]
  3.4 0.7 copy.17.target
  4.2 0.8 reduce
  5.0 0.1 maximum_maximum_fusion.tok_ref
  5.1 0.0 copy-start.1
  5.1 0.0 copy-start.2
  5.1 0.0 copy-start.5
  5.1 2.9 %gather_pages.1 = (bf16[4,64,256]{2,1,0:T(8,128)(2,1)}, bf16[16,64,256]{2,1,0:T(8,128)(2,1)}) custom-call(s32[1]{0:T(128)} %bitcast.where, s32[8,16]{1,0:T(8,128)} %dtable.3, s32[1,32]{1,0:T(1,128)} %ptable.3, s32[16,1]{1,0:T(8,128)} %copy.15.migrant, bf16[160,1,64,256]{3,2,1,0:T(8,128)(2,1)} %pool_ref.3), custom_call_target="tpu_custom_call" | custom-call | tf_op jit(solution)/shard_map/gather_pages/pallas_call | solution.py:234
  8.0 0.0 copy-start.6
  8.0 0.0 copy-start.7
  8.0 0.0 copy-start.8
  8.1 0.0 copy-start.9
  8.1 0.0 copy-done.1
  8.1 0.0 copy-done.2
  8.1 0.0 copy-start.3
  8.1 1.0 copy-done.3
  9.1 0.0 copy-start.4
  9.1 0.9 copy-done.4
  10.0 71.2 %prefill_exchange.1 = (bf16[128,8192]{1,0:T(8,128)(2,1)S(1)}, bf16[1024,256]{1,0:T(8,128)(2,1)S(1)}, bf16[16,8,16,128]{3,2,1,0:T(8,128)(2,1)S(1)}, bf16[16,256,256]{2,1,0:T(8,128)(2,1)S(1)}) custom-call(s32[1]{0:T(128)S(6)} %copy.22.prefix, bf16[128,8192]{1,0:T(8,128)(2,1)S(1)} %copy-done.1, bf16[128,2048]{1,0:T(8,128)(2,1)S(1)} %copy-done.2, ...), custom_call_target="tpu_custom_call" | custom-call | tf_op jit(solution)/shard_map/prefill_exchange/pallas_call | solution.py:194
  81.2 0.0 copy-done.5
  81.2 0.0 copy-done.6
  81.2 0.0 copy-done.7
  81.3 0.0 copy-done.8
  81.3 0.0 copy-done.9
  81.3 0.0 copy-start
  81.3 2.5 %copy-done = bf16[160,1,64,256]{3,2,1,0:T(8,128)(2,1)S(1)} copy-done((bf16[160,1,64,256]{3,2,1,0:T(8,128)(2,1)S(1)}, bf16[160,1,64,256]{3,2,1,0:T(8,128)(2,1)}, u32[]{:S(2)}) %copy-start) | copy-done | bytes 5242904
  83.8 18.5 %decode_and_pool.1 = (bf16[8,8,128]{2,1,0:T(8,128)(2,1)S(1)}, bf16[160,1,64,256]{3,2,1,0:T(8,128)(2,1)}) custom-call(s32[1]{0:T(128)} %bitcast.where, s32[8,16]{1,0:T(8,128)S(1)} %copy-done.6, s32[1,32]{1,0:T(1,128)S(1)} %copy-done.7, s32[128]{0:T(128)S(1)} %copy-done.8, s32[16,1]{1,0:T(8,128)S(1)} %copy-done.5, s32[16,1]{1,0:T(8,128)S(1)} %copy.17.target, ...), custom_call_target="tpu_custom_call" | custom-call | flops 33554432 | bytes 11534336 | tf_op jit(solution)/shard_map/decode_and_pool/pallas_call | solution.py:352
  102.3 0.6 copy.20
  102.9 1.3 %copy.23 = bf16[128,8192]{1,0:T(8,128)(2,1)} copy(bf16[128,8192]{1,0:T(8,128)(2,1)S(1)} %get-tuple-element.22) | data formatting | bytes 4194304
  (1 shorter events, 0.0 us)
Async XLA Ops:
  5.1 3.0 %copy-start.1 = (bf16[128,8192]{1,0:T(8,128)(2,1)S(1)}, bf16[128,8192]{1,0:T(8,128)(2,1)}, u32[]{:S(2)}) copy-start(bf16[128,8192]{1,0:T(8,128)(2,1)} %q_ref.1) | copy-start | bytes 6291460
  5.1 3.0 %copy-start.2 = (bf16[128,2048]{1,0:T(8,128)(2,1)S(1)}, bf16[128,2048]{1,0:T(8,128)(2,1)}, u32[]{:S(2)}) copy-start(bf16[128,2048]{1,0:T(8,128)(2,1)} %pair_ref.1) | copy-start | bytes 1572868
  5.1 76.1 %copy-start.5 = (s32[16,1]{1,0:T(8,128)S(1)}, s32[16,1]{1,0:T(8,128)}, u32[]{:S(2)}) copy-start(s32[16,1]{1,0:T(8,128)} %copy.15.migrant) | copy-start | bytes 196
  8.0 73.2 %copy-start.6 = (s32[8,16]{1,0:T(8,128)S(1)}, s32[8,16]{1,0:T(8,128)}, u32[]{:S(2)}) copy-start(s32[8,16]{1,0:T(8,128)} %dtable.3) | copy-start | bytes 1540
  8.0 73.2 %copy-start.7 = (s32[1,32]{1,0:T(1,128)S(1)}, s32[1,32]{1,0:T(1,128)}, u32[]{:S(2)}) copy-start(s32[1,32]{1,0:T(1,128)} %ptable.3) | copy-start | bytes 388
  8.0 73.2 %copy-start.8 = (s32[128]{0:T(128)S(1)}, s32[128]{0:T(128)}, u32[]{:S(2)}) copy-start(s32[128]{0:T(128)} %cached.1) | copy-start | bytes 1540
  8.1 73.2 %copy-start.9 = (s32[128]{0:T(128)S(1)}, s32[128]{0:T(128)}, u32[]{:S(2)}) copy-start(s32[128]{0:T(128)} %arrivals.1) | copy-start | bytes 1540
  8.1 1.0 %copy-start.3 = (bf16[16,64,256]{2,1,0:T(8,128)(2,1)S(1)}, bf16[16,64,256]{2,1,0:T(8,128)(2,1)}, u32[]{:S(2)}) copy-start(bf16[16,64,256]{2,1,0:T(8,128)(2,1)} %get-tuple-element.12) | copy-start | bytes 1572868
  9.1 0.9 copy-start.4
  81.3 2.5 %copy-start = (bf16[160,1,64,256]{3,2,1,0:T(8,128)(2,1)S(1)}, bf16[160,1,64,256]{3,2,1,0:T(8,128)(2,1)}, u32[]{:S(2)}) copy-start(bf16[160,1,64,256]{3,2,1,0:T(8,128)(2,1)} %pool_ref.3) | copy-start | bytes 15728644

commit v4 on v3

--- a/solution.py
+++ b/solution.py
@@ -139,7 +139,7 @@
                 used = spare + 256 * (case + 1)
                 row0 = (src % 2) * block
 
-                @pl.loop(0, QPK // 2)
+                @pl.loop(0, QPK // 2, unroll=2)
                 def _(pair):
                     c0 = pl.multiple_of(pair * 2 * HD, 2 * HD)
                     c1 = pl.multiple_of(pair * 2 * HD + HD, HD)

time: 105 us -> 96 us (0.914)
  Pallas kernels: 92.6 us -> 84 us
    pallas_call x1, Pallas kernels: 71.2 us -> 62.6 us  [prefill(): pl.pallas_call(prefill_kernel, out_shape=(jax.ShapeDtypeStruct((block, co...]
where the time goes in v4:
time: 96 us; the launch traced here: 95.6 us
  Pallas kernels  84 us (88%)
  local copies, waits for them, and re-layouts  8.53 us (9%)
  other arithmetic  1.65 us (2%)
  between operations  1.43 us (1%)
    pallas_call x1, Pallas kernels, prefill(): pl.pallas_call(prefill_kernel, out_shape=(jax.ShapeDtypeStruct((block, co...  62.6 us
    pallas_call x1, Pallas kernels, decode_and_store(): pl.pallas_call(decode_kernel, out_shape=(jax.ShapeDtypeStruct((slots, QPK...  18.5 us
    unnamed x24, local copies, waits for them, and re-layouts  8.45 us
    pallas_call x1, Pallas kernels, gather(): pl.pallas_call(gather_kernel, out_shape=tuple((jax.ShapeDtypeStruct((n, P...  2.91 us

profile of v4, /device:TPU:0, one launch (start us, length us, event | category | flops | bytes accessed | tf_op | source)
XLA Modules:
  0.0 95.6 jit_solution(17073497125212668230)
XLA Ops:
  1.3 0.1 pad.2.clone
  1.4 0.7 reduce.1
  2.1 1.3 %copy.15.migrant = s32[16,1]{1,0:T(8,128)} copy(s32[16,1]{0,1:T(1,128)} %param.21) | data formatting | bytes 128 | tf_op args[9]
  3.4 0.7 copy.17.target
  4.2 0.8 reduce
  5.0 0.1 maximum_maximum_fusion.tok_ref
  5.1 0.0 copy-start.1
  5.1 0.0 copy-start.2
  5.1 0.0 copy-start.5
  5.1 2.9 %gather_pages.1 = (bf16[4,64,256]{2,1,0:T(8,128)(2,1)}, bf16[16,64,256]{2,1,0:T(8,128)(2,1)}) custom-call(s32[1]{0:T(128)} %bitcast.where, s32[8,16]{1,0:T(8,128)} %dtable.3, s32[1,32]{1,0:T(1,128)} %ptable.3, s32[16,1]{1,0:T(8,128)} %copy.15.migrant, bf16[160,1,64,256]{3,2,1,0:T(8,128)(2,1)} %pool_ref.3), custom_call_target="tpu_custom_call" | custom-call | tf_op jit(solution)/shard_map/gather_pages/pallas_call | solution.py:234
  8.0 0.0 copy-start.6
  8.0 0.0 copy-start.7
  8.0 0.0 copy-start.8
  8.1 0.0 copy-start.9
  8.1 0.0 copy-done.1
  8.1 0.0 copy-done.2
  8.1 0.0 copy-start.3
  8.1 1.0 %copy-done.3 = bf16[16,64,256]{2,1,0:T(8,128)(2,1)S(1)} copy-done((bf16[16,64,256]{2,1,0:T(8,128)(2,1)S(1)}, bf16[16,64,256]{2,1,0:T(8,128)(2,1)}, u32[]{:S(2)}) %copy-start.3) | copy-done | bytes 524312
  9.1 0.0 copy-start.4
  9.1 0.9 copy-done.4
  10.0 62.6 %prefill_exchange.1 = (bf16[128,8192]{1,0:T(8,128)(2,1)S(1)}, bf16[1024,256]{1,0:T(8,128)(2,1)S(1)}, bf16[16,8,16,128]{3,2,1,0:T(8,128)(2,1)S(1)}, bf16[16,256,256]{2,1,0:T(8,128)(2,1)S(1)}) custom-call(s32[1]{0:T(128)S(6)} %copy.22.prefix, bf16[128,8192]{1,0:T(8,128)(2,1)S(1)} %copy-done.1, bf16[128,2048]{1,0:T(8,128)(2,1)S(1)} %copy-done.2, ...), custom_call_target="tpu_custom_call" | custom-call | tf_op jit(solution)/shard_map/prefill_exchange/pallas_call | solution.py:194
  72.6 0.0 copy-done.5
  72.6 0.0 copy-done.6
  72.6 0.0 copy-done.7
  72.6 0.0 copy-done.8
  72.6 0.0 copy-done.9
  72.6 0.0 copy-start
  72.7 2.5 %copy-done = bf16[160,1,64,256]{3,2,1,0:T(8,128)(2,1)S(1)} copy-done((bf16[160,1,64,256]{3,2,1,0:T(8,128)(2,1)S(1)}, bf16[160,1,64,256]{3,2,1,0:T(8,128)(2,1)}, u32[]{:S(2)}) %copy-start) | copy-done | bytes 5242904
  75.1 18.5 %decode_and_pool.1 = (bf16[8,8,128]{2,1,0:T(8,128)(2,1)S(1)}, bf16[160,1,64,256]{3,2,1,0:T(8,128)(2,1)}) custom-call(s32[1]{0:T(128)} %bitcast.where, s32[8,16]{1,0:T(8,128)S(1)} %copy-done.6, s32[1,32]{1,0:T(1,128)S(1)} %copy-done.7, s32[128]{0:T(128)S(1)} %copy-done.8, s32[16,1]{1,0:T(8,128)S(1)} %copy-done.5, s32[16,1]{1,0:T(8,128)S(1)} %copy.17.target, ...), custom_call_target="tpu_custom_call" | custom-call | flops 33554432 | bytes 11534336 | tf_op jit(solution)/shard_map/decode_and_pool/pallas_call | solution.py:352
  93.6 0.6 copy.20
  94.3 1.3 %copy.23 = bf16[128,8192]{1,0:T(8,128)(2,1)} copy(bf16[128,8192]{1,0:T(8,128)(2,1)S(1)} %get-tuple-element.22) | data formatting | bytes 4194304
  (1 shorter events, 0.0 us)
Async XLA Ops:
  5.1 3.0 %copy-start.1 = (bf16[128,8192]{1,0:T(8,128)(2,1)S(1)}, bf16[128,8192]{1,0:T(8,128)(2,1)}, u32[]{:S(2)}) copy-start(bf16[128,8192]{1,0:T(8,128)(2,1)} %q_ref.1) | copy-start | bytes 6291460
  5.1 3.0 %copy-start.2 = (bf16[128,2048]{1,0:T(8,128)(2,1)S(1)}, bf16[128,2048]{1,0:T(8,128)(2,1)}, u32[]{:S(2)}) copy-start(bf16[128,2048]{1,0:T(8,128)(2,1)} %pair_ref.1) | copy-start | bytes 1572868
  5.1 67.5 %copy-start.5 = (s32[16,1]{1,0:T(8,128)S(1)}, s32[16,1]{1,0:T(8,128)}, u32[]{:S(2)}) copy-start(s32[16,1]{1,0:T(8,128)} %copy.15.migrant) | copy-start | bytes 196
  8.0 64.6 %copy-start.6 = (s32[8,16]{1,0:T(8,128)S(1)}, s32[8,16]{1,0:T(8,128)}, u32[]{:S(2)}) copy-start(s32[8,16]{1,0:T(8,128)} %dtable.3) | copy-start | bytes 1540
  8.0 64.6 %copy-start.7 = (s32[1,32]{1,0:T(1,128)S(1)}, s32[1,32]{1,0:T(1,128)}, u32[]{:S(2)}) copy-start(s32[1,32]{1,0:T(1,128)} %ptable.3) | copy-start | bytes 388
  8.0 64.6 %copy-start.8 = (s32[128]{0:T(128)S(1)}, s32[128]{0:T(128)}, u32[]{:S(2)}) copy-start(s32[128]{0:T(128)} %cached.1) | copy-start | bytes 1540
  8.1 64.6 %copy-start.9 = (s32[128]{0:T(128)S(1)}, s32[128]{0:T(128)}, u32[]{:S(2)}) copy-start(s32[128]{0:T(128)} %arrivals.1) | copy-start | bytes 1540
  8.1 1.0 %copy-start.3 = (bf16[16,64,256]{2,1,0:T(8,128)(2,1)S(1)}, bf16[16,64,256]{2,1,0:T(8,128)(2,1)}, u32[]{:S(2)}) copy-start(bf16[16,64,256]{2,1,0:T(8,128)(2,1)} %get-tuple-element.12) | copy-start | bytes 1572868
  9.1 0.9 copy-start.4
  72.6 2.5 %copy-start = (bf16[160,1,64,256]{3,2,1,0:T(8,128)(2,1)S(1)}, bf16[160,1,64,256]{3,2,1,0:T(8,128)(2,1)}, u32[]{:S(2)}) copy-start(bf16[160,1,64,256]{3,2,1,0:T(8,128)(2,1)} %pool_ref.3) | copy-start | bytes 15728644
